TPU v7x, 512 devices: a whole 4x8x8 slice. The times are simulated.
512 devices in a mesh: row: 8 (over x, core), col: 64 (over z, y).
Axes of the slice: x: 4, y: 8, z: 8, core: 2. Of those that a mesh axis runs over, the one named last changes fastest.
Arguments:
- src_latent: bfloat16 [32, 32768], P(None, 'row'), may hold values from -6 to 6
- tgt_latent: bfloat16 [32, 131072], P(None, 'col'), may hold values from -6 to 6
- g_start: float32 [131072], P('col'), may hold values from -1.5 to 1.5
- pairs: int32 [8, 64, 8, 2], P('row', 'col'), may hold values from 0 to 7, as said below
- counts: int32 [8, 64], P('row', 'col'), may hold values from 1 to 8, as said below
Outputs:
- f_new: float32 [32768], P('row')
- g_new: float32 [131072], P('col')
- bary: float32 [32, 32768], P(None, 'row')
Inputs may be any that keep to these rules, and one draw needn't show every extreme that they name: Within one device's 8 slots all pairs are distinct; entry 0 is below 8 and entry 1 below 4. Every source block and every target block appears among the live slots of some device. `counts`: some device has exactly 8 live slots in every draw.
All inputs are finite; a program needn't handle non-finite values.
Results may differ from a plain program's by a relative error of at most 0.0012.
Values sent between devices are 32-bit elements; how exact they have to be, the bound alone decides.
No kernel may reach another device: no remote copies, remote signals or barrier semaphores. Data moves between devices by JAX's collectives and lax.ppermute only.
A program may use at most 64 MiB of HBM per device.

v0:
```python
import jax
import jax.numpy as jnp
from jax import lax
from jax.sharding import PartitionSpec as P

BLOCK = 512


epsilon = 0.01
very_low = -1e30


def body(src_latent, tgt_latent, g_start, pairs, counts):
    src_len = src_latent.shape[1]
    tgt_len = tgt_latent.shape[1]
    width = src_latent.shape[0]
    rows_all = src_len * lax.axis_size("row")
    cols_all = tgt_len * lax.axis_size("col")
    sq_src = jnp.sum(jnp.square(src_latent.astype(jnp.float32)), axis=0)
    sq_tgt = jnp.sum(jnp.square(tgt_latent.astype(jnp.float32)), axis=0)
    slots = pairs[0, 0]
    count = counts[0, 0]

    def tile_score(p, row_pot, col_pot):
        s_off = slots[p, 0] * BLOCK
        t_off = slots[p, 1] * BLOCK
        xs = lax.dynamic_slice_in_dim(src_latent, s_off, BLOCK, 1)
        ys = lax.dynamic_slice_in_dim(tgt_latent, t_off, BLOCK, 1)
        cross = lax.dot_general(
            xs, ys, (((0,), (0,)), ((), ())), preferred_element_type=jnp.float32
        )
        sx = lax.dynamic_slice_in_dim(sq_src, s_off, BLOCK)
        sy = lax.dynamic_slice_in_dim(sq_tgt, t_off, BLOCK)
        cost = (sx[:, None] + sy[None, :] - 2.0 * cross) / width
        shifted = -cost
        if row_pot is not None:
            shifted = shifted + lax.dynamic_slice_in_dim(row_pot, s_off, BLOCK)[:, None]
        if col_pot is not None:
            shifted = shifted + lax.dynamic_slice_in_dim(col_pot, t_off, BLOCK)[None, :]
        return (shifted / epsilon, s_off, t_off, ys)

    def expand(vec, axis):
        return vec[:, None] if axis == 1 else vec[None, :]

    def local_peak(row_pot, col_pot, axis, length):

        def step(p, peak):
            score, s_off, t_off, _ = tile_score(p, row_pot, col_pot)
            off = s_off if axis == 1 else t_off
            old = lax.dynamic_slice_in_dim(peak, off, BLOCK)
            return lax.dynamic_update_slice_in_dim(
                peak, jnp.maximum(old, jnp.max(score, axis=axis)), off, 0
            )

        return lax.fori_loop(0, count, step, jnp.full((length,), very_low, jnp.float32))

    def local_total(row_pot, col_pot, axis, length, peak):

        def step(p, total):
            score, s_off, t_off, _ = tile_score(p, row_pot, col_pot)
            off = s_off if axis == 1 else t_off
            top = expand(lax.dynamic_slice_in_dim(peak, off, BLOCK), axis)
            old = lax.dynamic_slice_in_dim(total, off, BLOCK)
            return lax.dynamic_update_slice_in_dim(
                total, old + jnp.sum(jnp.exp(score - top), axis=axis), off, 0
            )

        return lax.fori_loop(0, count, step, jnp.zeros((length,), jnp.float32))

    peak_f = lax.pmax(local_peak(None, g_start, 1, src_len), "col")
    total_f = lax.psum(local_total(None, g_start, 1, src_len, peak_f), "col")
    f_new = -epsilon * jnp.log(1.0 * rows_all) - epsilon * (peak_f + jnp.log(total_f))
    peak_g = lax.pmax(local_peak(f_new, None, 0, tgt_len), "row")
    total_g = lax.psum(local_total(f_new, None, 0, tgt_len, peak_g), "row")
    g_new = -epsilon * jnp.log(1.0 * cols_all) - epsilon * (peak_g + jnp.log(total_g))
    peak_b = lax.pmax(local_peak(None, g_new, 1, src_len), "col")

    def accumulate(p, carry):
        numer, denom = carry
        score, s_off, t_off, ys = tile_score(p, None, g_new)
        top = lax.dynamic_slice_in_dim(peak_b, s_off, BLOCK)
        weight = jnp.exp(score - top[:, None]).astype(jnp.bfloat16)
        part = lax.dot_general(
            ys, weight, (((1,), (1,)), ((), ())), preferred_element_type=jnp.float32
        )
        old = lax.dynamic_slice_in_dim(numer, s_off, BLOCK, 1)
        numer = lax.dynamic_update_slice_in_dim(numer, old + part, s_off, 1)
        old_den = lax.dynamic_slice_in_dim(denom, s_off, BLOCK)
        denom = lax.dynamic_update_slice_in_dim(
            denom, old_den + jnp.sum(weight.astype(jnp.float32), axis=1), s_off, 0
        )
        return (numer, denom)

    init = (jnp.zeros((width, src_len), jnp.float32), jnp.zeros((src_len,), jnp.float32))
    numer, denom = lax.fori_loop(0, count, accumulate, init)
    numer, denom = lax.psum((numer, denom), "col")
    bary = numer / denom[None, :]
    return (f_new, g_new, bary)


def solution(mesh):
    in_specs = (
        P(None, "row"),
        P(None, "col"),
        P("col"),
        P("row", "col", None, None),
        P("row", "col"),
    )
    out_specs = (P("row"), P("col"), P(None, "row"))
    return jax.shard_map(body, mesh=mesh, in_specs=in_specs, out_specs=out_specs, check_vma=False)
```

profile of v0, /device:TPU:262, one launch (start us, length us, event | category | flops | bytes accessed | tf_op | source)
XLA Modules:
  0.0 1292.4 jit_solution(17436968615771430454)
XLA Ops:
  7.2 1.0 multiply_reduce_fusion.1
  8.2 1.1 multiply_reduce_fusion
  9.3 0.6 copy-done.1
  10.0 4.1 while.62
  10.7 0.7 constant_dynamic-slice_fusion.18
  14.1 297.5 %pmax.21 = f32[4096]{0:T(1024)S(1)} all-reduce(f32[4096]{0:T(1024)S(1)} %get-tuple-element.312), channel_id=1, replica_groups=mesh['row'=8,'col'=64] {'col'}, use_global_device_ids=true, to_apply=%region_5.0 | all-reduce | flops 4096 | bytes 32768 | tf_op jit(solution)/shard_map/pmax | solution.py:70
  311.6 4.3 while.63
  312.3 0.7 constant_dynamic-slice_fusion.19
  315.9 295.8 %psum.28 = f32[4096]{0:T(1024)S(1)} all-reduce(f32[4096]{0:T(1024)S(1)} %get-tuple-element.313), channel_id=1, replica_groups=mesh['row'=8,'col'=64] {'col'}, use_global_device_ids=true, to_apply=%region_9.0 | all-reduce | flops 4096 | bytes 32768 | tf_op jit(solution)/shard_map/psum | solution.py:71
  611.7 4.1 while.64
  612.4 0.6 constant_dynamic-slice_fusion.20
  615.8 25.6 %pmax.22 = f32[2048]{0:T(1024)S(1)} all-reduce(f32[2048]{0:T(1024)S(1)} %get-tuple-element.314), channel_id=1, replica_groups=mesh['row'=8,'col'=64] {'row'}, use_global_device_ids=true, to_apply=%region_13.0 | all-reduce | flops 2048 | bytes 16384 | tf_op jit(solution)/shard_map/pmax | solution.py:73
  641.4 4.3 while.65
  642.1 0.6 constant_dynamic-slice_fusion.21
  645.7 33.0 %psum.29 = f32[2048]{0:T(1024)S(1)} all-reduce(f32[2048]{0:T(1024)S(1)} %get-tuple-element.315), channel_id=1, replica_groups=mesh['row'=8,'col'=64] {'row'}, use_global_device_ids=true, to_apply=%region_17.0 | all-reduce | flops 2048 | bytes 16384 | tf_op jit(solution)/shard_map/psum | solution.py:74
  678.8 4.1 while.66
  679.4 0.6 constant_dynamic-slice_fusion.22
  682.9 298.7 %pmax.23 = f32[4096]{0:T(1024)S(1)} all-reduce(f32[4096]{0:T(1024)S(1)} %get-tuple-element.316), channel_id=1, replica_groups=mesh['row'=8,'col'=64] {'col'}, use_global_device_ids=true, to_apply=%region_21.0 | all-reduce | flops 4096 | bytes 32768 | tf_op jit(solution)/shard_map/pmax | solution.py:76
  981.6 4.5 while.67
  982.2 0.6 constant_dynamic-slice_fusion.23
  984.5 0.6 convert_reduce_fusion.2
  986.1 0.8 copy-done
  986.9 296.8 %psum.31 = f32[4096]{0:T(1024)S(1)} all-reduce(f32[4096]{0:T(1024)S(1)} %get-tuple-element.318), channel_id=1, replica_groups=mesh['row'=8,'col'=64] {'col'}, use_global_device_ids=true, to_apply=%region_26.0 | all-reduce | flops 4096 | bytes 32768 | tf_op jit(solution)/shard_map/psum | solution.py:96
  1283.7 1.9 broadcast_divide_fusion
  (57 shorter events, 5.6 us)
Async XLA Ops:
  7.2 2.2 copy-start.3
  7.2 1276.5 %all-reduce.2.cloned.1.call-start = ((), (), s32[]{:S(2)}) async-start(), calls=%async_computation | async-start | bytes 1048576 | tf_op jit(solution)/shard_map/psum | solution.py:96
  8.2 1.1 copy-start.2
  9.3 0.7 copy-start.1
  9.3 0.7 copy-start.6
  645.7 33.1 %copy-start.5 = (f32[4096]{0:T(1024)}, f32[4096]{0:T(1024)S(1)}, u32[]{:S(2)}) copy-start(f32[4096]{0:T(1024)S(1)} %get-tuple-element.1153) | copy-start | bytes 49156
  986.1 0.8 copy-start
  986.1 0.8 copy-start.4
Sparse Core Ops, SparseCore 0:
  987.0 171.5 all-reduce.1
where the time goes:
time: 1290 us
  blocking collectives  1250 us (97%)
  loops' own time  15.7 us (1%)
  between operations  14.2 us (1%)
    pmax x1, blocking collectives, body(): peak_b = lax.pmax(local_peak(None, g_new, 1, src_len), 'col')  299 us
    pmax x1, blocking collectives, body(): peak_f = lax.pmax(local_peak(None, g_start, 1, src_len), 'col')  297 us
    psum x1, blocking collectives, body(): numer, denom = lax.psum((numer, denom), 'col')  297 us
    psum x1, blocking collectives, body(): total_f = lax.psum(local_total(None, g_start, 1, src_len, peak_f), 'col')  296 us
    psum x1, blocking collectives, body(): total_g = lax.psum(local_total(f_new, None, 0, tgt_len, peak_g), 'row')  33 us
  transfers between devices with their start and end apart: 1, of which 0 were waited for; matrix products, arithmetic and copies ran while one was open for 0% of the time, Pallas kernels for 0%

commit v1 on v0

v1 whole, which is shorter than its diff:
```python
import functools
import math

import jax
import jax.numpy as jnp
from jax import lax
from jax.experimental import pallas as pl
from jax.experimental.pallas import tpu as pltpu
from jax.sharding import PartitionSpec as P

BLOCK = 512
LANES = 128
DIM = 32
DEPTH = 80

epsilon = 0.01
very_low = -1e30
cross_scale = 2.0 / (DIM * epsilon)
square_scale = 1.0 / (DIM * epsilon)

F32 = jnp.float32
BF16 = jnp.bfloat16


def pieces(vec):
    first = vec.astype(BF16).astype(F32)
    rest = vec - first
    second = rest.astype(BF16).astype(F32)
    return first, second, rest - second


def bias_rows(vec):
    row = lax.broadcasted_iota(jnp.int32, (16, vec.shape[1]), 0)
    a, b, c = pieces(vec)
    return jnp.where(row == 0, a, jnp.where(row == 1, b, jnp.where(row == 2, c, 0.0))).astype(BF16)


def one_rows(width):
    row = lax.broadcasted_iota(jnp.int32, (16, width), 0)
    return jnp.where(row < 3, 1.0, 0.0).astype(BF16)


def fill_src(x_ref, xa):
    for b in range(xa.shape[0]):
        xs = x_ref[:, b * BLOCK : (b + 1) * BLOCK].astype(F32) * cross_scale
        high = xs.astype(BF16)
        xa[b, 0:32, :] = high
        xa[b, 32:64, :] = (xs - high.astype(F32)).astype(BF16)


def fill_tgt(y_ref, ya):
    for b in range(ya.shape[0]):
        ys = y_ref[:, b * BLOCK : (b + 1) * BLOCK]
        ya[b, 0:32, :] = ys
        ya[b, 32:64, :] = ys


def tile_scores(left, right):
    return lax.dot_general(left, right, (((0,), (0,)), ((), ())), preferred_element_type=F32)


def online(score, top_ref, total_ref, at):
    old = top_ref[at]
    top = jnp.maximum(old, jnp.max(score, axis=0, keepdims=True))
    weight = jnp.exp(score - top)
    keep = jnp.exp(old - top)
    total_ref[at] = total_ref[at] * keep + jnp.sum(weight, axis=0, keepdims=True)
    top_ref[at] = top


def clear(top_ref, total_ref):
    top_ref[...] = jnp.full(top_ref.shape, very_low, F32)
    total_ref[...] = jnp.zeros(total_ref.shape, F32)


def spread_rows(top_ref, total_ref, out_ref, copies):
    per = BLOCK // LANES
    rows = top_ref.shape[0] * per
    for b in range(top_ref.shape[0]):
        total = total_ref[b]
        lse = jnp.where(total > 0.0, top_ref[b] + jnp.log(total), very_low)
        for k in range(per):
            out_ref[b * per + k : b * per + k + 1, :] = lse[:, k * LANES : (k + 1) * LANES]
    value = out_ref[0:rows, :]
    for c in range(1, copies):
        out_ref[c * rows : (c + 1) * rows, :] = value


def merged(in_ref, parts):
    rows = in_ref.shape[0] // parts
    values = [in_ref[c * rows : (c + 1) * rows, :] for c in range(parts)]
    top = functools.reduce(jnp.maximum, values)
    total = functools.reduce(jnp.add, [jnp.exp(v - top) for v in values])
    return top + jnp.log(total)


def src_kernel(parts, slots, count, x_ref, y_ref, g_ref, out_ref, xa, ya, top_ref, total_ref):
    fill_src(x_ref, xa)
    fill_tgt(y_ref, ya)
    for b in range(xa.shape[0]):
        xa[b, 64:80, :] = one_rows(BLOCK)
    for b in range(ya.shape[0]):
        ys = y_ref[:, b * BLOCK : (b + 1) * BLOCK].astype(F32)
        square = jnp.sum(ys * ys, axis=0, keepdims=True)
        start = g_ref[:, b * BLOCK : (b + 1) * BLOCK]
        ya[b, 64:80, :] = bias_rows(start / epsilon - square * square_scale)
    clear(top_ref, total_ref)

    def step(p, carry):
        s, t = slots[2 * p], slots[2 * p + 1]
        online(tile_scores(ya[t], xa[s]), top_ref, total_ref, s)
        return carry

    lax.fori_loop(0, count[0], step, 0)
    spread_rows(top_ref, total_ref, out_ref, parts)


def merge_kernel(parts, in_ref, out_ref):
    value = merged(in_ref, parts)
    rows = value.shape[0]
    for c in range(parts):
        out_ref[c * rows : (c + 1) * rows, :] = value


def tgt_kernel(parts, copies, log_rows, slots, count, in_ref, x_ref, y_ref, f_ref, out_ref, xa, ya, top_ref, total_ref):
    fill_src(x_ref, xa)
    fill_tgt(y_ref, ya)
    for b in range(ya.shape[0]):
        ya[b, 64:80, :] = one_rows(BLOCK)
    bias = -log_rows - merged(in_ref, parts)
    per = BLOCK // LANES
    for b in range(xa.shape[0]):
        xs = x_ref[:, b * BLOCK : (b + 1) * BLOCK].astype(F32)
        square = jnp.sum(xs * xs, axis=0, keepdims=True)
        for k in range(per):
            row = b * per + k
            lanes = slice(k * LANES, (k + 1) * LANES)
            one = bias[row : row + 1, :]
            xa[b, 64:80, lanes] = bias_rows(one)
            f_ref[row : row + 1, :] = epsilon * one + square[:, lanes] * (1.0 / DIM)
    clear(top_ref, total_ref)

    def step(p, carry):
        s, t = slots[2 * p], slots[2 * p + 1]
        online(tile_scores(xa[s], ya[t]), top_ref, total_ref, t)
        return carry

    lax.fori_loop(0, count[0], step, 0)
    spread_rows(top_ref, total_ref, out_ref, copies)


def bary_kernel(parts, log_cols, slots, count, in_ref, x_ref, y_ref, g_ref, out_ref, xa, ya, yb, top_ref, acc_ref):
    fill_src(x_ref, xa)
    fill_tgt(y_ref, ya)
    for b in range(xa.shape[0]):
        xa[b, 64:80, :] = one_rows(BLOCK)
    bias = -log_cols - merged(in_ref, parts)
    per = BLOCK // LANES
    first_row = lax.broadcasted_iota(jnp.int32, (16, BLOCK), 0) == 0
    for b in range(ya.shape[0]):
        y_block = y_ref[:, b * BLOCK : (b + 1) * BLOCK]
        ys = y_block.astype(F32)
        square = jnp.sum(ys * ys, axis=0, keepdims=True)
        yb[b, 0:32, :] = y_block
        yb[b, 32:48, :] = jnp.where(first_row, 1.0, 0.0).astype(BF16)
        for k in range(per):
            row = b * per + k
            lanes = slice(k * LANES, (k + 1) * LANES)
            one = bias[row : row + 1, :]
            ya[b, 64:80, lanes] = bias_rows(one)
            g_ref[row : row + 1, :] = epsilon * one + square[:, lanes] * (1.0 / DIM)
    top_ref[...] = jnp.full(top_ref.shape, very_low, F32)
    acc_ref[...] = jnp.zeros(acc_ref.shape, F32)

    def step(p, carry):
        s, t = slots[2 * p], slots[2 * p + 1]
        score = tile_scores(ya[t], xa[s])
        old = top_ref[s]
        top = jnp.maximum(old, jnp.max(score, axis=0, keepdims=True))
        weight = jnp.exp(score - top).astype(BF16)
        part = jnp.dot(yb[t], weight, preferred_element_type=F32)
        acc_ref[s] = acc_ref[s] * jnp.exp(old - top) + part
        top_ref[s] = top
        return carry

    lax.fori_loop(0, count[0], step, 0)
    for b in range(top_ref.shape[0]):
        total = acc_ref[b, 32:33, :]
        live = total > 0.0
        lse = jnp.where(live, top_ref[b] + jnp.log(total), very_low)
        mean = acc_ref[b, 0:32, :] * jnp.where(live, 1.0 / total, 0.0)
        for k in range(per):
            lanes = slice(k * LANES, (k + 1) * LANES)
            for h in range(2):
                at = ((b * per + k) * 2 + h) * 17
                out_ref[at : at + 16, :] = mean[h * 16 : h * 16 + 16, lanes]
                out_ref[at + 16 : at + 17, :] = lse[:, lanes]


def mean_kernel(parts, in_ref, out_ref):
    logs = [in_ref[c * 17 + 16 : c * 17 + 17, :] for c in range(parts)]
    top = functools.reduce(jnp.maximum, logs)
    total = jnp.zeros_like(top)
    value = jnp.zeros((16, LANES), F32)
    for c in range(parts):
        weight = jnp.exp(logs[c] - top)
        total = total + weight
        value = value + weight * in_ref[c * 17 : c * 17 + 16, :]
    value = value / total
    for c in range(parts):
        out_ref[c * 16 : (c + 1) * 16, :] = value


def place_kernel(in_ref, out_ref):
    for c in range(in_ref.shape[0] // 16):
        k, h = c // 2, c % 2
        out_ref[h * 16 : (h + 1) * 16, k * LANES : (k + 1) * LANES] = in_ref[c * 16 : (c + 1) * 16, :]


def whole(count):
    return [pl.BlockSpec(memory_space=pltpu.VMEM)] * count


def scalars():
    return [pl.BlockSpec(memory_space=pltpu.SMEM)] * 2


def body(src_latent, tgt_latent, g_start, pairs, counts):
    src_len = src_latent.shape[1]
    tgt_len = tgt_latent.shape[1]
    n_row, n_col = lax.axis_size("row"), lax.axis_size("col")
    side = 8
    other = n_col // side
    groups_z = [[z * side + y for z in range(other)] for y in range(side)]
    groups_y = [[z * side + y for y in range(side)] for z in range(other)]
    slots = pairs.reshape(-1)
    count = counts.reshape(-1)
    s_blocks, t_blocks = src_len // BLOCK, tgt_len // BLOCK
    s_rows, t_rows = src_len // LANES, tgt_len // LANES
    log_rows = math.log(src_len * n_row)
    log_cols = math.log(tgt_len * n_col)

    def aug(blocks):
        return pltpu.VMEM((blocks, DEPTH, BLOCK), BF16)

    def line(blocks):
        return pltpu.VMEM((blocks, 1, BLOCK), F32)

    def exchange(x, axis, parts, groups=None):
        width = x.shape[0] // parts * LANES
        y = lax.all_to_all(
            x.reshape(parts, width), axis, 0, 0, axis_index_groups=groups, tiled=True
        )
        return y.reshape(-1, LANES)

    def rows_of(n):
        return jax.ShapeDtypeStruct((n, LANES), F32)

    lse = pl.pallas_call(
        functools.partial(src_kernel, other),
        out_shape=rows_of(other * s_rows),
        in_specs=scalars() + whole(3),
        out_specs=whole(1)[0],
        scratch_shapes=[aug(s_blocks), aug(t_blocks), line(s_blocks), line(s_blocks)],
        name="src_pass",
    )(slots, count, src_latent, tgt_latent, g_start.reshape(1, -1))
    lse = exchange(lse, "col", other, groups_z)
    lse = pl.pallas_call(
        functools.partial(merge_kernel, other),
        out_shape=rows_of(side * s_rows),
        in_specs=whole(1),
        out_specs=whole(1)[0],
        name="src_merge",
    )(lse)
    lse = exchange(lse, "col", side, groups_y)
    f_new, lse = pl.pallas_call(
        functools.partial(tgt_kernel, side, n_row, log_rows),
        out_shape=(rows_of(s_rows), rows_of(n_row * t_rows)),
        in_specs=scalars() + whole(3),
        out_specs=tuple(whole(2)),
        scratch_shapes=[aug(s_blocks), aug(t_blocks), line(t_blocks), line(t_blocks)],
        name="tgt_pass",
    )(slots, count, lse, src_latent, tgt_latent)
    lse = exchange(lse, "row", n_row)
    g_new, means = pl.pallas_call(
        functools.partial(bary_kernel, n_row, log_cols),
        out_shape=(rows_of(t_rows), rows_of(n_col * 17)),
        in_specs=scalars() + whole(3),
        out_specs=tuple(whole(2)),
        scratch_shapes=[
            aug(s_blocks),
            aug(t_blocks),
            pltpu.VMEM((t_blocks, 48, BLOCK), BF16),
            line(s_blocks),
            pltpu.VMEM((s_blocks, 48, BLOCK), F32),
        ],
        name="bary_pass",
    )(slots, count, lse, src_latent, tgt_latent)
    means = exchange(means, "col", n_col)
    means = pl.pallas_call(
        functools.partial(mean_kernel, n_col),
        out_shape=rows_of(n_col * 16),
        in_specs=whole(1),
        out_specs=whole(1)[0],
        name="bary_merge",
    )(means)
    means = exchange(means, "col", n_col)
    bary = pl.pallas_call(
        place_kernel,
        out_shape=jax.ShapeDtypeStruct((DIM, src_len), F32),
        in_specs=whole(1),
        out_specs=whole(1)[0],
        name="bary_place",
    )(means)
    return f_new.reshape(-1), g_new.reshape(-1), bary


def solution(mesh):
    in_specs = (
        P(None, "row"),
        P(None, "col"),
        P("col"),
        P("row", "col", None, None),
        P("row", "col"),
    )
    out_specs = (P("row"), P("col"), P(None, "row"))
    return jax.shard_map(body, mesh=mesh, in_specs=in_specs, out_specs=out_specs, check_vma=False)
```

time: 1290 us -> 118 us (0.09)
  the two profiles are of different devices: /device:TPU:262 before, /device:TPU:2 now
where the time goes in v1:
time: 118 us; the launch traced here: 117 us
  blocking collectives  96.9 us (82%)
  Pallas kernels  18 us (15%)
  between operations  1.3 us (1%)
    all_to_all x5, blocking collectives, exchange(): lax.all_to_all(x.reshape(parts, width), axis, 0, 0, axis_index_groups=gro...  96.9 us
    pallas_call x1, Pallas kernels, body(): pl.pallas_call(functools.partial(bary_kernel, n_row, log_cols), out_shape...  4.6 us
    pallas_call x1, Pallas kernels, body(): pl.pallas_call(functools.partial(src_kernel, other), out_shape=rows_of(ot...  3.92 us
    pallas_call x1, Pallas kernels, body(): pl.pallas_call(functools.partial(tgt_kernel, side, n_row, log_rows), out_...  3.92 us

profile of v1, /device:TPU:2, one launch (start us, length us, event | category | flops | bytes accessed | tf_op | source)
XLA Modules:
  0.0 116.9 jit_solution(2331633659140283910)
XLA Ops:
  0.6 0.0 copy-start
  1.3 0.0 copy-done
  1.3 0.1 copy.10
  1.4 0.6 reshape.61.slots
  2.0 3.9 %src_pass.1 = f32[256,128]{1,0:T(8,128)} custom-call(s32[16]{0:T(128)} %reshape.61.slots, s32[1]{0:T(128)} %bitcast.16.count, bf16[32,4096]{1,0:T(8,128)(2,1)} %x_ref.5, bf16[32,2048]{1,0:T(8,128)(2,1)} %y_ref.5, f32[1,2048]{1,0:T(1,128)} %bitcast.29), custom_call_target="tpu_custom_call" | custom-call | tf_op jit(solution)/shard_map/src_pass/pallas_call | solution.py:259
  6.0 21.0 %all_to_all.45 = f32[8,1,4096]{2,1,0:T(1,128)} all-to-all(f32[8,1,4096]{2,1,0:T(1,128)} %bitcast.26), channel_id=1, replica_groups={{0,8,16,24,32,40,48,56},{1,9,17,25,33,41,49,57},{2,10,18,26,34,42,50,58..., dimensions={0} | all-to-all | bytes 262144 | tf_op jit(solution)/shard_map/all_to_all | solution.py:251
  26.9 1.6 %src_merge.1 = f32[256,128]{1,0:T(8,128)} custom-call(f32[256,128]{1,0:T(8,128)} %bitcast.23), custom_call_target="tpu_custom_call" | custom-call | tf_op jit(solution)/shard_map/src_merge/pallas_call | solution.py:268
  28.6 16.2 %all_to_all.46 = f32[8,1,4096]{2,1,0:T(1,128)} all-to-all(f32[8,1,4096]{2,1,0:T(1,128)} %bitcast.24), channel_id=1, replica_groups={{0,1,2,3,4,5,6,7},{8,9,10,11,12,13,14,15},{16,17,18,19,20,21,22,23},{24..., dimensions={0} | all-to-all | bytes 262144 | tf_op jit(solution)/shard_map/all_to_all | solution.py:251
  44.8 3.9 %tgt_pass.1 = (f32[32,128]{1,0:T(8,128)}, f32[128,128]{1,0:T(8,128)}) custom-call(s32[16]{0:T(128)} %reshape.61.slots, s32[1]{0:T(128)} %bitcast.17.count, f32[256,128]{1,0:T(8,128)} %bitcast.25, bf16[32,4096]{1,0:T(8,128)(2,1)} %x_ref.5, bf16[32,2048]{1,0:T(8,128)(2,1)} %y_ref.5), custom_call_target="tpu_custom_call" | custom-call | tf_op jit(solution)/shard_map/tgt_pass/pallas_call | solution.py:276
  48.7 9.1 %all_to_all.47 = f32[8,1,2048]{2,1,0:T(1,128)} all-to-all(f32[8,1,2048]{2,1,0:T(1,128)} %bitcast.28), channel_id=1, replica_groups=mesh['row'=8,'col'=64] {'row'}, dimensions={0} | all-to-all | bytes 131072 | tf_op jit(solution)/shard_map/all_to_all | solution.py:251
  57.9 4.6 %bary_pass.1 = (f32[16,128]{1,0:T(8,128)}, f32[1088,128]{1,0:T(8,128)}) custom-call(s32[16]{0:T(128)} %reshape.61.slots, s32[1]{0:T(128)} %bitcast.18.count, f32[128,128]{1,0:T(8,128)} %bitcast.27, bf16[32,4096]{1,0:T(8,128)(2,1)} %x_ref.5, bf16[32,2048]{1,0:T(8,128)(2,1)} %y_ref.5), custom_call_target="tpu_custom_call" | custom-call | tf_op jit(solution)/shard_map/bary_pass/pallas_call | solution.py:285
  62.5 26.6 %all_to_all.48 = f32[64,1,2176]{2,1,0:T(1,128)} all-to-all(f32[64,1,2176]{2,1,0:T(1,128)} %bitcast.22), channel_id=1, replica_groups=mesh['row'=8,'col'=64] {'col'}, dimensions={0} | all-to-all | bytes 1114112 | tf_op jit(solution)/shard_map/all_to_all | solution.py:251
  89.1 2.0 %bary_merge.1 = f32[1024,128]{1,0:T(8,128)} custom-call(f32[1088,128]{1,0:T(8,128)} %bitcast.19), custom_call_target="tpu_custom_call" | custom-call | tf_op jit(solution)/shard_map/bary_merge/pallas_call | solution.py:300
  91.1 24.0 %all_to_all.49 = f32[64,1,2048]{2,1,0:T(1,128)} all-to-all(f32[64,1,2048]{2,1,0:T(1,128)} %bitcast.20), channel_id=1, replica_groups=mesh['row'=8,'col'=64] {'col'}, dimensions={0} | all-to-all | bytes 1048576 | tf_op jit(solution)/shard_map/all_to_all | solution.py:251
  115.1 1.9 %bary_place.1 = f32[32,4096]{1,0:T(8,128)} custom-call(f32[1024,128]{1,0:T(8,128)} %bitcast.21), custom_call_target="tpu_custom_call" | custom-call | tf_op jit(solution)/shard_map/bary_place/pallas_call | solution.py:308
Async XLA Ops:
  0.6 0.7 copy-start

commit v2 on v1

--- a/solution.py
+++ b/solution.py
@@ -12,6 +12,8 @@
 LANES = 128
 DIM = 32
 DEPTH = 80
+PACK = 18
+VMEM_LIMIT = 16 * 2**20
 
 epsilon = 0.01
 very_low = -1e30
@@ -107,11 +109,11 @@
     clear(top_ref, total_ref)
 
     def step(p, carry):
-        s, t = slots[2 * p], slots[2 * p + 1]
+        s, t = slots[0, p], slots[1, p]
         online(tile_scores(ya[t], xa[s]), top_ref, total_ref, s)
         return carry
 
-    lax.fori_loop(0, count[0], step, 0)
+    lax.fori_loop(0, count[0, 0], step, 0)
     spread_rows(top_ref, total_ref, out_ref, parts)
 
 
@@ -141,11 +143,11 @@
     clear(top_ref, total_ref)
 
     def step(p, carry):
-        s, t = slots[2 * p], slots[2 * p + 1]
+        s, t = slots[0, p], slots[1, p]
         online(tile_scores(xa[s], ya[t]), top_ref, total_ref, t)
         return carry
 
-    lax.fori_loop(0, count[0], step, 0)
+    lax.fori_loop(0, count[0, 0], step, 0)
     spread_rows(top_ref, total_ref, out_ref, copies)
 
 
@@ -173,7 +175,7 @@
     acc_ref[...] = jnp.zeros(acc_ref.shape, F32)
 
     def step(p, carry):
-        s, t = slots[2 * p], slots[2 * p + 1]
+        s, t = slots[0, p], slots[1, p]
         score = tile_scores(ya[t], xa[s])
         old = top_ref[s]
         top = jnp.maximum(old, jnp.max(score, axis=0, keepdims=True))
@@ -183,38 +185,37 @@
         top_ref[s] = top
         return carry
 
-    lax.fori_loop(0, count[0], step, 0)
+    lax.fori_loop(0, count[0, 0], step, 0)
     for b in range(top_ref.shape[0]):
         total = acc_ref[b, 32:33, :]
         live = total > 0.0
         lse = jnp.where(live, top_ref[b] + jnp.log(total), very_low)
         mean = acc_ref[b, 0:32, :] * jnp.where(live, 1.0 / total, 0.0)
-        for k in range(per):
-            lanes = slice(k * LANES, (k + 1) * LANES)
-            for h in range(2):
-                at = ((b * per + k) * 2 + h) * 17
-                out_ref[at : at + 16, :] = mean[h * 16 : h * 16 + 16, lanes]
-                out_ref[at + 16 : at + 17, :] = lse[:, lanes]
+        for h in range(DIM // 8):
+            for k in range(per):
+                lanes = slice(k * LANES, (k + 1) * LANES)
+                owner = (h * top_ref.shape[0] * per + b * per + k) // 2
+                at = owner * PACK + k % 2 * 8
+                out_ref[at : at + 8, :] = mean[h * 8 : h * 8 + 8, lanes]
+                at = owner * PACK + 16 + k % 2
+                out_ref[at : at + 1, :] = lse[:, lanes]
 
 
 def mean_kernel(parts, in_ref, out_ref):
-    logs = [in_ref[c * 17 + 16 : c * 17 + 17, :] for c in range(parts)]
-    top = functools.reduce(jnp.maximum, logs)
-    total = jnp.zeros_like(top)
-    value = jnp.zeros((16, LANES), F32)
-    for c in range(parts):
-        weight = jnp.exp(logs[c] - top)
-        total = total + weight
-        value = value + weight * in_ref[c * 17 : c * 17 + 16, :]
-    value = value / total
-    for c in range(parts):
-        out_ref[c * 16 : (c + 1) * 16, :] = value
-
-
-def place_kernel(in_ref, out_ref):
-    for c in range(in_ref.shape[0] // 16):
-        k, h = c // 2, c % 2
-        out_ref[h * 16 : (h + 1) * 16, k * LANES : (k + 1) * LANES] = in_ref[c * 16 : (c + 1) * 16, :]
+    for half in range(2):
+        logs = [in_ref[c * PACK + 16 + half : c * PACK + 17 + half, :] for c in range(parts)]
+        top = functools.reduce(jnp.maximum, logs)
+        total = jnp.zeros_like(top)
+        value = jnp.zeros((8, LANES), F32)
+        for c in range(parts):
+            weight = jnp.exp(logs[c] - top)
+            total = total + weight
+            at = c * PACK + half * 8
+            value = value + weight * in_ref[at : at + 8, :]
+        value = value / total
+        for c in range(parts):
+            at = c * 16 + half * 8
+            out_ref[at : at + 8, :] = value
 
 
 def whole(count):
@@ -233,8 +234,8 @@
     other = n_col // side
     groups_z = [[z * side + y for z in range(other)] for y in range(side)]
     groups_y = [[z * side + y for y in range(side)] for z in range(other)]
-    slots = pairs.reshape(-1)
-    count = counts.reshape(-1)
+    slots = pairs.reshape(pairs.shape[2:]).T
+    count = counts
     s_blocks, t_blocks = src_len // BLOCK, tgt_len // BLOCK
     s_rows, t_rows = src_len // LANES, tgt_len // LANES
     log_rows = math.log(src_len * n_row)
@@ -262,6 +263,7 @@
         in_specs=scalars() + whole(3),
         out_specs=whole(1)[0],
         scratch_shapes=[aug(s_blocks), aug(t_blocks), line(s_blocks), line(s_blocks)],
+        compiler_params=pltpu.CompilerParams(vmem_limit_bytes=VMEM_LIMIT),
         name="src_pass",
     )(slots, count, src_latent, tgt_latent, g_start.reshape(1, -1))
     lse = exchange(lse, "col", other, groups_z)
@@ -270,6 +272,7 @@
         out_shape=rows_of(side * s_rows),
         in_specs=whole(1),
         out_specs=whole(1)[0],
+        compiler_params=pltpu.CompilerParams(vmem_limit_bytes=VMEM_LIMIT),
         name="src_merge",
     )(lse)
     lse = exchange(lse, "col", side, groups_y)
@@ -279,12 +282,13 @@
         in_specs=scalars() + whole(3),
         out_specs=tuple(whole(2)),
         scratch_shapes=[aug(s_blocks), aug(t_blocks), line(t_blocks), line(t_blocks)],
+        compiler_params=pltpu.CompilerParams(vmem_limit_bytes=VMEM_LIMIT),
         name="tgt_pass",
     )(slots, count, lse, src_latent, tgt_latent)
     lse = exchange(lse, "row", n_row)
     g_new, means = pl.pallas_call(
         functools.partial(bary_kernel, n_row, log_cols),
-        out_shape=(rows_of(t_rows), rows_of(n_col * 17)),
+        out_shape=(rows_of(t_rows), rows_of(n_col * PACK)),
         in_specs=scalars() + whole(3),
         out_specs=tuple(whole(2)),
         scratch_shapes=[
@@ -294,6 +298,7 @@
             line(s_blocks),
             pltpu.VMEM((s_blocks, 48, BLOCK), F32),
         ],
+        compiler_params=pltpu.CompilerParams(vmem_limit_bytes=VMEM_LIMIT),
         name="bary_pass",
     )(slots, count, lse, src_latent, tgt_latent)
     means = exchange(means, "col", n_col)
@@ -302,16 +307,12 @@
         out_shape=rows_of(n_col * 16),
         in_specs=whole(1),
         out_specs=whole(1)[0],
+        compiler_params=pltpu.CompilerParams(vmem_limit_bytes=VMEM_LIMIT),
         name="bary_merge",
     )(means)
     means = exchange(means, "col", n_col)
-    bary = pl.pallas_call(
-        place_kernel,
-        out_shape=jax.ShapeDtypeStruct((DIM, src_len), F32),
-        in_specs=whole(1),
-        out_specs=whole(1)[0],
-        name="bary_place",
-    )(means)
+    tiles = means.reshape(DIM // 8, s_rows, 8, LANES)
+    bary = tiles.transpose(0, 2, 1, 3).reshape(DIM, src_len)
     return f_new.reshape(-1), g_new.reshape(-1), bary
 
 

time: 118 us -> 112 us (0.949)
  the two profiles are of different devices: /device:TPU:2 before, /device:TPU:8 now
where the time goes in v2:
time: 112 us; the launch traced here: 110 us
  blocking collectives  99.4 us (89%)
  Pallas kernels  5.42 us (5%)
  local copies, waits for them, and re-layouts  4.02 us (4%)
  between operations  1.3 us (1%)
    all_to_all x5, blocking collectives, exchange(): lax.all_to_all(x.reshape(parts, width), axis, 0, 0, axis_index_groups=gro...  99.4 us
    unnamed x11, local copies, waits for them, and re-layouts  4.02 us

profile of v2, /device:TPU:8, one launch (start us, length us, event | category | flops | bytes accessed | tf_op | source)
XLA Modules:
  0.0 110.2 jit_solution(6550069757653654859)
XLA Ops:
  1.3 0.0 copy-start.3
  1.3 0.7 copy-done.3
  2.0 0.0 copy-start
  2.0 0.9 copy-done
  2.9 0.0 copy-start.2
  2.9 0.9 copy-done.2
  3.8 0.0 copy-start.4
  3.8 0.7 copy-done.4
  4.5 1.3 %src_pass.1 = f32[256,128]{1,0:T(8,128)S(1)} custom-call(s32[2,8]{1,0:T(2,128)S(1)} %bitcast.29, s32[1,1]{1,0:T(1,128)S(6)} %copy.14.count, bf16[32,4096]{1,0:T(8,128)(2,1)S(1)} %copy-done, bf16[32,2048]{1,0:T(8,128)(2,1)S(1)} %copy-done.2, f32[1,2048]{1,0:T(1,128)S(1)} %bitcast.32), custom_call_target="tpu_custom_call" | custom-call | tf_op jit(solution)/shard_map/src_pass/pallas_call | solution.py:260
  5.8 22.2 %all_to_all.45 = f32[8,1,4096]{2,1,0:T(1,128)S(1)} all-to-all(f32[8,1,4096]{2,1,0:T(1,128)S(1)} %bitcast.24), channel_id=1, replica_groups={{0,8,16,24,32,40,48,56},{1,9,17,25,33,41,49,57},{2,10,18,26,34,42,50,58..., dimensions={0} | all-to-all | bytes 262144 | tf_op jit(solution)/shard_map/all_to_all | solution.py:252
  28.0 0.0 copy-start.1
  28.0 15.1 %all_to_all.46 = f32[8,1,4096]{2,1,0:T(1,128)S(1)} all-to-all(f32[8,1,4096]{2,1,0:T(1,128)S(1)} %bitcast.26), channel_id=1, replica_groups={{0,1,2,3,4,5,6,7},{8,9,10,11,12,13,14,15},{16,17,18,19,20,21,22,23},{24..., dimensions={0} | all-to-all | bytes 262144 | tf_op jit(solution)/shard_map/all_to_all | solution.py:252
  43.1 0.0 copy-done.1
  43.1 1.9 %tgt_pass.1 = (f32[32,128]{1,0:T(8,128)}, f32[128,128]{1,0:T(8,128)S(1)}) custom-call(s32[2,8]{1,0:T(2,128)S(1)} %bitcast.30, s32[1,1]{1,0:T(1,128)S(6)} %copy.14.count, f32[256,128]{1,0:T(8,128)S(1)} %bitcast.23, bf16[32,4096]{1,0:T(8,128)(2,1)S(1)} %copy-done.1, bf16[32,2048]{1,0:T(8,128)(2,1)S(1)} %copy-done.2), custom_call_target="tpu_custom_call" | custom-call | tf_op jit(solution)/shard_map/tgt_pass/pallas_call | solution.py:279
  45.0 11.4 %all_to_all.47 = f32[8,1,2048]{2,1,0:T(1,128)S(1)} all-to-all(f32[8,1,2048]{2,1,0:T(1,128)S(1)} %bitcast.28), channel_id=1, replica_groups=mesh['row'=8,'col'=64] {'row'}, dimensions={0} | all-to-all | bytes 131072 | tf_op jit(solution)/shard_map/all_to_all | solution.py:252
  56.4 2.0 %bary_pass.1 = (f32[16,128]{1,0:T(8,128)}, f32[1152,128]{1,0:T(8,128)S(1)}) custom-call(s32[2,8]{1,0:T(2,128)S(1)} %bitcast.31, s32[1,1]{1,0:T(1,128)S(6)} %copy.14.count, f32[128,128]{1,0:T(8,128)S(1)} %bitcast.27, bf16[32,4096]{1,0:T(8,128)(2,1)S(1)} %copy-done.1, bf16[32,2048]{1,0:T(8,128)(2,1)S(1)} %copy-done.2), custom_call_target="tpu_custom_call" | custom-call | tf_op jit(solution)/shard_map/bary_pass/pallas_call | solution.py:289
  58.4 27.7 %all_to_all.48 = f32[64,1,2304]{2,1,0:T(1,128)S(1)} all-to-all(f32[64,1,2304]{2,1,0:T(1,128)S(1)} %bitcast.22), channel_id=1, replica_groups=mesh['row'=8,'col'=64] {'col'}, dimensions={0} | all-to-all | bytes 1179648 | tf_op jit(solution)/shard_map/all_to_all | solution.py:252
  86.0 0.2 bary_merge.1
  86.3 23.1 %all_to_all.49 = f32[64,1,2048]{2,1,0:T(1,128)S(1)} all-to-all(f32[64,1,2048]{2,1,0:T(1,128)S(1)} %bitcast.21), channel_id=1, replica_groups=mesh['row'=8,'col'=64] {'col'}, dimensions={0} | all-to-all | bytes 1048576 | tf_op jit(solution)/shard_map/all_to_all | solution.py:252
  109.4 0.8 copy.15
  (1 shorter events, 0.0 us)
Async XLA Ops:
  1.3 0.7 copy-start.3
  2.0 0.9 copy-start
  2.9 0.9 copy-start.2
  3.8 0.7 copy-start.4
  28.0 15.1 %copy-start.1 = (bf16[32,4096]{1,0:T(8,128)(2,1)S(1)}, bf16[32,4096]{1,0:T(8,128)(2,1)}, u32[]{:S(2)}) copy-start(bf16[32,4096]{1,0:T(8,128)(2,1)} %x_ref.5) | copy-start | bytes 786436

commit v3 on v2

--- a/solution.py
+++ b/solution.py
@@ -11,14 +11,16 @@
 BLOCK = 512
 LANES = 128
 DIM = 32
-DEPTH = 80
+DEPTH = 112
 PACK = 18
 VMEM_LIMIT = 16 * 2**20
 
 epsilon = 0.01
 very_low = -1e30
-cross_scale = 2.0 / (DIM * epsilon)
-square_scale = 1.0 / (DIM * epsilon)
+log2e = math.log2(math.e)
+unit = epsilon / log2e
+cross_scale = 2.0 / (DIM * unit)
+square_scale = 1.0 / (DIM * unit)
 
 F32 = jnp.float32
 BF16 = jnp.bfloat16
@@ -45,29 +47,67 @@
 def fill_src(x_ref, xa):
     for b in range(xa.shape[0]):
         xs = x_ref[:, b * BLOCK : (b + 1) * BLOCK].astype(F32) * cross_scale
-        high = xs.astype(BF16)
-        xa[b, 0:32, :] = high
-        xa[b, 32:64, :] = (xs - high.astype(F32)).astype(BF16)
+        for k, piece in enumerate(pieces(xs)):
+            xa[b, k * DIM : (k + 1) * DIM, :] = piece.astype(BF16)
 
 
 def fill_tgt(y_ref, ya):
     for b in range(ya.shape[0]):
         ys = y_ref[:, b * BLOCK : (b + 1) * BLOCK]
-        ya[b, 0:32, :] = ys
-        ya[b, 32:64, :] = ys
+        for k in range(3):
+            ya[b, k * DIM : (k + 1) * DIM, :] = ys
 
 
 def tile_scores(left, right):
     return lax.dot_general(left, right, (((0,), (0,)), ((), ())), preferred_element_type=F32)
 
 
-def online(score, top_ref, total_ref, at):
+CHUNK = 128
+
+
+UNROLL = 2
+
+
+def tile_lse(left, right):
+    top = total = None
+    scores = tile_scores(left, right)
+    for c in range(0, BLOCK, CHUNK):
+        score = scores[c : c + CHUNK, :].reshape(CHUNK // 8, 8, BLOCK)
+        most = jnp.max(score, axis=0)
+        old, top = top, most if c == 0 else jnp.maximum(top, most)
+        part = jnp.sum(jnp.exp2(score - top), axis=0)
+        total = part if c == 0 else total * jnp.exp2(old - top) + part
+    return top, total
+
+
+def add_tile(tile, top_ref, total_ref, at):
+    top, total = tile
     old = top_ref[at]
-    top = jnp.maximum(old, jnp.max(score, axis=0, keepdims=True))
-    weight = jnp.exp(score - top)
-    keep = jnp.exp(old - top)
-    total_ref[at] = total_ref[at] * keep + jnp.sum(weight, axis=0, keepdims=True)
-    top_ref[at] = top
+    most = jnp.maximum(old, top)
+    total_ref[at] = total_ref[at] * jnp.exp2(old - most) + total * jnp.exp2(top - most)
+    top_ref[at] = most
+
+
+def lse_tiles(count, slots, left_of, right_of, at_of, spare, top_ref, total_ref):
+    def step(q, carry):
+        tiles = []
+        for u in range(UNROLL):
+            p = q * UNROLL + u
+            live = p < count
+            p = jnp.minimum(p, count - 1)
+            s, t = slots[0, p], slots[1, p]
+            tiles.append((tile_lse(left_of(s, t), right_of(s, t)), jnp.where(live, at_of(s, t), spare)))
+        for tile, at in tiles:
+            add_tile(tile, top_ref, total_ref, at)
+        return carry
+
+    lax.fori_loop(0, lax.div(count + UNROLL - 1, UNROLL), step, 0)
+
+
+def joined(top, total):
+    most = jnp.max(top, axis=0, keepdims=True)
+    total = jnp.sum(total * jnp.exp2(top - most), axis=0, keepdims=True)
+    return jnp.where(total > 0.0, most + jnp.log2(total), very_low)
 
 
 def clear(top_ref, total_ref):
@@ -75,12 +115,11 @@
     total_ref[...] = jnp.zeros(total_ref.shape, F32)
 
 
-def spread_rows(top_ref, total_ref, out_ref, copies):
+def spread_rows(blocks, top_ref, total_ref, out_ref, copies):
     per = BLOCK // LANES
-    rows = top_ref.shape[0] * per
-    for b in range(top_ref.shape[0]):
-        total = total_ref[b]
-        lse = jnp.where(total > 0.0, top_ref[b] + jnp.log(total), very_low)
+    rows = blocks * per
+    for b in range(blocks):
+        lse = joined(top_ref[b], total_ref[b])
         for k in range(per):
             out_ref[b * per + k : b * per + k + 1, :] = lse[:, k * LANES : (k + 1) * LANES]
     value = out_ref[0:rows, :]
@@ -92,29 +131,48 @@
     rows = in_ref.shape[0] // parts
     values = [in_ref[c * rows : (c + 1) * rows, :] for c in range(parts)]
     top = functools.reduce(jnp.maximum, values)
-    total = functools.reduce(jnp.add, [jnp.exp(v - top) for v in values])
-    return top + jnp.log(total)
-
-
-def src_kernel(parts, slots, count, x_ref, y_ref, g_ref, out_ref, xa, ya, top_ref, total_ref):
+    total = functools.reduce(jnp.add, [jnp.exp2(v - top) for v in values])
+    return top + jnp.log2(total)
+
+
+def fetch(sources, targets, sems):
+    copies = [
+        pltpu.make_async_copy(source, target, sems.at[k])
+        for k, (source, target) in enumerate(zip(sources, targets))
+    ]
+    for copy in copies:
+        copy.start()
+    return copies
+
+
+def src_kernel(parts, count, slots_in, x_in, y_in, g_in, out_ref, slots, x_ref, y_ref, g_ref, sems, xa, ya, top_ref, total_ref):
+    copies = fetch(
+        (x_in, y_in, g_in, slots_in), (x_ref, y_ref, g_ref, slots), sems
+    )
+    for b in range(xa.shape[0]):
+        xa[b, 3 * DIM : DEPTH, :] = one_rows(BLOCK)
+    clear(top_ref, total_ref)
+    for copy in copies:
+        copy.wait()
     fill_src(x_ref, xa)
     fill_tgt(y_ref, ya)
-    for b in range(xa.shape[0]):
-        xa[b, 64:80, :] = one_rows(BLOCK)
     for b in range(ya.shape[0]):
         ys = y_ref[:, b * BLOCK : (b + 1) * BLOCK].astype(F32)
         square = jnp.sum(ys * ys, axis=0, keepdims=True)
         start = g_ref[:, b * BLOCK : (b + 1) * BLOCK]
-        ya[b, 64:80, :] = bias_rows(start / epsilon - square * square_scale)
-    clear(top_ref, total_ref)
-
-    def step(p, carry):
-        s, t = slots[0, p], slots[1, p]
-        online(tile_scores(ya[t], xa[s]), top_ref, total_ref, s)
-        return carry
-
-    lax.fori_loop(0, count[0, 0], step, 0)
-    spread_rows(top_ref, total_ref, out_ref, parts)
+        ya[b, 3 * DIM : DEPTH, :] = bias_rows(start / unit - square * square_scale)
+
+    lse_tiles(
+        count[0, 0],
+        slots,
+        lambda s, t: ya[t],
+        lambda s, t: xa[s],
+        lambda s, t: s,
+        xa.shape[0],
+        top_ref,
+        total_ref,
+    )
+    spread_rows(xa.shape[0], top_ref, total_ref, out_ref, parts)
 
 
 def merge_kernel(parts, in_ref, out_ref):
@@ -128,7 +186,7 @@
     fill_src(x_ref, xa)
     fill_tgt(y_ref, ya)
     for b in range(ya.shape[0]):
-        ya[b, 64:80, :] = one_rows(BLOCK)
+        ya[b, 3 * DIM : DEPTH, :] = one_rows(BLOCK)
     bias = -log_rows - merged(in_ref, parts)
     per = BLOCK // LANES
     for b in range(xa.shape[0]):
@@ -138,24 +196,28 @@
             row = b * per + k
             lanes = slice(k * LANES, (k + 1) * LANES)
             one = bias[row : row + 1, :]
-            xa[b, 64:80, lanes] = bias_rows(one)
-            f_ref[row : row + 1, :] = epsilon * one + square[:, lanes] * (1.0 / DIM)
+            xa[b, 3 * DIM : DEPTH, lanes] = bias_rows(one)
+            f_ref[row : row + 1, :] = unit * one + square[:, lanes] * (1.0 / DIM)
     clear(top_ref, total_ref)
 
-    def step(p, carry):
-        s, t = slots[0, p], slots[1, p]
-        online(tile_scores(xa[s], ya[t]), top_ref, total_ref, t)
-        return carry
-
-    lax.fori_loop(0, count[0, 0], step, 0)
-    spread_rows(top_ref, total_ref, out_ref, copies)
+    lse_tiles(
+        count[0, 0],
+        slots,
+        lambda s, t: xa[s],
+        lambda s, t: ya[t],
+        lambda s, t: t,
+        ya.shape[0],
+        top_ref,
+        total_ref,
+    )
+    spread_rows(ya.shape[0], top_ref, total_ref, out_ref, copies)
 
 
 def bary_kernel(parts, log_cols, slots, count, in_ref, x_ref, y_ref, g_ref, out_ref, xa, ya, yb, top_ref, acc_ref):
     fill_src(x_ref, xa)
     fill_tgt(y_ref, ya)
     for b in range(xa.shape[0]):
-        xa[b, 64:80, :] = one_rows(BLOCK)
+        xa[b, 3 * DIM : DEPTH, :] = one_rows(BLOCK)
     bias = -log_cols - merged(in_ref, parts)
     per = BLOCK // LANES
     first_row = lax.broadcasted_iota(jnp.int32, (16, BLOCK), 0) == 0
@@ -169,32 +231,47 @@
             row = b * per + k
             lanes = slice(k * LANES, (k + 1) * LANES)
             one = bias[row : row + 1, :]
-            ya[b, 64:80, lanes] = bias_rows(one)
-            g_ref[row : row + 1, :] = epsilon * one + square[:, lanes] * (1.0 / DIM)
+            ya[b, 3 * DIM : DEPTH, lanes] = bias_rows(one)
+            g_ref[row : row + 1, :] = unit * one + square[:, lanes] * (1.0 / DIM)
     top_ref[...] = jnp.full(top_ref.shape, very_low, F32)
     acc_ref[...] = jnp.zeros(acc_ref.shape, F32)
 
-    def step(p, carry):
-        s, t = slots[0, p], slots[1, p]
-        score = tile_scores(ya[t], xa[s])
-        old = top_ref[s]
-        top = jnp.maximum(old, jnp.max(score, axis=0, keepdims=True))
-        weight = jnp.exp(score - top).astype(BF16)
-        part = jnp.dot(yb[t], weight, preferred_element_type=F32)
-        acc_ref[s] = acc_ref[s] * jnp.exp(old - top) + part
-        top_ref[s] = top
+    spare = xa.shape[0]
+
+    def step(q, carry):
+        tiles = []
+        for u in range(2):
+            p = q * 2 + u
+            live = p < count[0, 0]
+            p = jnp.minimum(p, count[0, 0] - 1)
+            s, t = slots[0, p], slots[1, p]
+            scores = tile_scores(ya[t], xa[s])
+            top = part = None
+            for c in range(0, BLOCK, 128):
+                score = scores[c : c + 128, :]
+                most = jnp.max(score, axis=0, keepdims=True)
+                old, top = top, most if c == 0 else jnp.maximum(top, most)
+                weight = jnp.exp2(score - top).astype(BF16)
+                more = jnp.dot(yb[t, :, c : c + 128], weight, preferred_element_type=F32)
+                part = more if c == 0 else part * jnp.exp2(old - top) + more
+            tiles.append((top, part, jnp.where(live, s, spare)))
+        for top, part, at in tiles:
+            old = top_ref[at]
+            most = jnp.maximum(old, top)
+            acc_ref[at] = acc_ref[at] * jnp.exp2(old - most) + part * jnp.exp2(top - most)
+            top_ref[at] = most
         return carry
 
-    lax.fori_loop(0, count[0, 0], step, 0)
-    for b in range(top_ref.shape[0]):
+    lax.fori_loop(0, lax.div(count[0, 0] + 2 - 1, 2), step, 0)
+    for b in range(spare):
         total = acc_ref[b, 32:33, :]
         live = total > 0.0
-        lse = jnp.where(live, top_ref[b] + jnp.log(total), very_low)
+        lse = jnp.where(live, top_ref[b] + jnp.log2(total), very_low)
         mean = acc_ref[b, 0:32, :] * jnp.where(live, 1.0 / total, 0.0)
         for h in range(DIM // 8):
             for k in range(per):
                 lanes = slice(k * LANES, (k + 1) * LANES)
-                owner = (h * top_ref.shape[0] * per + b * per + k) // 2
+                owner = (h * spare * per + b * per + k) // 2
                 at = owner * PACK + k % 2 * 8
                 out_ref[at : at + 8, :] = mean[h * 8 : h * 8 + 8, lanes]
                 at = owner * PACK + 16 + k % 2
@@ -208,7 +285,7 @@
         total = jnp.zeros_like(top)
         value = jnp.zeros((8, LANES), F32)
         for c in range(parts):
-            weight = jnp.exp(logs[c] - top)
+            weight = jnp.exp2(logs[c] - top)
             total = total + weight
             at = c * PACK + half * 8
             value = value + weight * in_ref[at : at + 8, :]
@@ -238,14 +315,14 @@
     count = counts
     s_blocks, t_blocks = src_len // BLOCK, tgt_len // BLOCK
     s_rows, t_rows = src_len // LANES, tgt_len // LANES
-    log_rows = math.log(src_len * n_row)
-    log_cols = math.log(tgt_len * n_col)
+    log_rows = math.log2(src_len * n_row)
+    log_cols = math.log2(tgt_len * n_col)
 
     def aug(blocks):
         return pltpu.VMEM((blocks, DEPTH, BLOCK), BF16)
 
-    def line(blocks):
-        return pltpu.VMEM((blocks, 1, BLOCK), F32)
+    def line(blocks, rows=8):
+        return pltpu.VMEM((blocks, rows, BLOCK), F32)
 
     def exchange(x, axis, parts, groups=None):
         width = x.shape[0] // parts * LANES
@@ -260,12 +337,21 @@
     lse = pl.pallas_call(
         functools.partial(src_kernel, other),
         out_shape=rows_of(other * s_rows),
-        in_specs=scalars() + whole(3),
+        in_specs=scalars()[:1] + [pl.BlockSpec(memory_space=pltpu.HBM)] * 4,
         out_specs=whole(1)[0],
-        scratch_shapes=[aug(s_blocks), aug(t_blocks), line(s_blocks), line(s_blocks)],
+        scratch_shapes=[
+            pltpu.SMEM(slots.shape, jnp.int32),
+            pltpu.VMEM(src_latent.shape, BF16),
+            pltpu.VMEM(tgt_latent.shape, BF16),
+            pltpu.VMEM((1, tgt_len), F32),
+            pltpu.SemaphoreType.DMA((4,)),
+            aug(s_blocks), aug(t_blocks), line(s_blocks + 1), line(s_blocks + 1)],
         compiler_params=pltpu.CompilerParams(vmem_limit_bytes=VMEM_LIMIT),
         name="src_pass",
-    )(slots, count, src_latent, tgt_latent, g_start.reshape(1, -1))
+    )(count, *[
+        pltpu.with_memory_space_constraint(a, pltpu.HBM)
+        for a in (slots, src_latent, tgt_latent, g_start.reshape(1, -1))
+    ])
     lse = exchange(lse, "col", other, groups_z)
     lse = pl.pallas_call(
         functools.partial(merge_kernel, other),
@@ -281,7 +367,7 @@
         out_shape=(rows_of(s_rows), rows_of(n_row * t_rows)),
         in_specs=scalars() + whole(3),
         out_specs=tuple(whole(2)),
-        scratch_shapes=[aug(s_blocks), aug(t_blocks), line(t_blocks), line(t_blocks)],
+        scratch_shapes=[aug(s_blocks), aug(t_blocks), line(t_blocks + 1), line(t_blocks + 1)],
         compiler_params=pltpu.CompilerParams(vmem_limit_bytes=VMEM_LIMIT),
         name="tgt_pass",
     )(slots, count, lse, src_latent, tgt_latent)
@@ -295,8 +381,8 @@
             aug(s_blocks),
             aug(t_blocks),
             pltpu.VMEM((t_blocks, 48, BLOCK), BF16),
-            line(s_blocks),
-            pltpu.VMEM((s_blocks, 48, BLOCK), F32),
+            line(s_blocks + 1, 1),
+            pltpu.VMEM((s_blocks + 1, 48, BLOCK), F32),
         ],
         compiler_params=pltpu.CompilerParams(vmem_limit_bytes=VMEM_LIMIT),
         name="bary_pass",

time: 112 us -> 108 us (0.964)
  the two profiles are of different devices: /device:TPU:8 before, /device:TPU:2 now
where the time goes in v3:
time: 108 us; the launch traced here: 107 us
  blocking collectives  95.3 us (88%)
  Pallas kernels  8.69 us (8%)
  local copies, waits for them, and re-layouts  1.48 us (1%)
  between operations  1.31 us (1%)
    all_to_all x5, blocking collectives, exchange(): lax.all_to_all(x.reshape(parts, width), axis, 0, 0, axis_index_groups=gro...  95.3 us
    pallas_call x1, Pallas kernels, body(): pl.pallas_call(functools.partial(bary_kernel, n_row, log_cols), out_shape...  3.28 us
    pallas_call x1, Pallas kernels, body(): pl.pallas_call(functools.partial(tgt_kernel, side, n_row, log_rows), out_...  2.59 us
    pallas_call x1, Pallas kernels, body(): pl.pallas_call(functools.partial(src_kernel, other), out_shape=rows_of(ot...  2.54 us

profile of v3, /device:TPU:2, one launch (start us, length us, event | category | flops | bytes accessed | tf_op | source)
XLA Modules:
  0.0 106.8 jit_solution(17793336772647977052)
XLA Ops:
  1.3 2.5 %src_pass.1 = f32[256,128]{1,0:T(8,128)S(1)} custom-call(s32[1,1]{1,0:T(1,128)S(6)} %copy.14.count, s32[2,8]{1,0:T(2,128)} %bitcast.29, bf16[32,4096]{1,0:T(8,128)(2,1)} %x_ref.3, bf16[32,2048]{1,0:T(8,128)(2,1)} %y_ref.3, f32[1,2048]{1,0:T(1,128)} %bitcast.33), custom_call_target="tpu_custom_call" | custom-call | tf_op jit(solution)/shard_map/src_pass/pallas_call | solution.py:337
  3.8 19.8 %all_to_all.45 = f32[8,1,4096]{2,1,0:T(1,128)S(1)} all-to-all(f32[8,1,4096]{2,1,0:T(1,128)S(1)} %bitcast.24), channel_id=1, replica_groups={{0,8,16,24,32,40,48,56},{1,9,17,25,33,41,49,57},{2,10,18,26,34,42,50,58..., dimensions={0} | all-to-all | bytes 262144 | tf_op jit(solution)/shard_map/all_to_all | solution.py:329
  23.6 0.0 copy-start
  23.6 0.0 copy-start.1
  23.6 16.7 %all_to_all.46 = f32[8,1,4096]{2,1,0:T(1,128)S(1)} all-to-all(f32[8,1,4096]{2,1,0:T(1,128)S(1)} %bitcast.26), channel_id=1, replica_groups={{0,1,2,3,4,5,6,7},{8,9,10,11,12,13,14,15},{16,17,18,19,20,21,22,23},{24..., dimensions={0} | all-to-all | bytes 262144 | tf_op jit(solution)/shard_map/all_to_all | solution.py:329
  40.3 0.0 copy-start.2
  40.4 0.0 copy-done
  40.4 0.0 copy-done.1
  40.4 0.7 copy-done.2
  41.0 2.6 %tgt_pass.1 = (f32[32,128]{1,0:T(8,128)}, f32[128,128]{1,0:T(8,128)S(1)}) custom-call(s32[2,8]{1,0:T(2,128)S(1)} %bitcast.30, s32[1,1]{1,0:T(1,128)S(6)} %copy.14.count, f32[256,128]{1,0:T(8,128)S(1)} %bitcast.23, bf16[32,4096]{1,0:T(8,128)(2,1)S(1)} %copy-done, bf16[32,2048]{1,0:T(8,128)(2,1)S(1)} %copy-done.1), custom_call_target="tpu_custom_call" | custom-call | tf_op jit(solution)/shard_map/tgt_pass/pallas_call | solution.py:365
  43.6 8.5 %all_to_all.47 = f32[8,1,2048]{2,1,0:T(1,128)S(1)} all-to-all(f32[8,1,2048]{2,1,0:T(1,128)S(1)} %bitcast.28), channel_id=1, replica_groups=mesh['row'=8,'col'=64] {'row'}, dimensions={0} | all-to-all | bytes 131072 | tf_op jit(solution)/shard_map/all_to_all | solution.py:329
  52.1 3.3 %bary_pass.1 = (f32[16,128]{1,0:T(8,128)}, f32[1152,128]{1,0:T(8,128)S(1)}) custom-call(s32[2,8]{1,0:T(2,128)S(1)} %bitcast.31, s32[1,1]{1,0:T(1,128)S(6)} %copy.14.count, f32[128,128]{1,0:T(8,128)S(1)} %bitcast.27, bf16[32,4096]{1,0:T(8,128)(2,1)S(1)} %copy-done, bf16[32,2048]{1,0:T(8,128)(2,1)S(1)} %copy-done.1), custom_call_target="tpu_custom_call" | custom-call | tf_op jit(solution)/shard_map/bary_pass/pallas_call | solution.py:375
  55.4 26.5 %all_to_all.48 = f32[64,1,2304]{2,1,0:T(1,128)S(1)} all-to-all(f32[64,1,2304]{2,1,0:T(1,128)S(1)} %bitcast.22), channel_id=1, replica_groups=mesh['row'=8,'col'=64] {'col'}, dimensions={0} | all-to-all | bytes 1179648 | tf_op jit(solution)/shard_map/all_to_all | solution.py:329
  81.9 0.2 bary_merge.1
  82.1 23.9 %all_to_all.49 = f32[64,1,2048]{2,1,0:T(1,128)S(1)} all-to-all(f32[64,1,2048]{2,1,0:T(1,128)S(1)} %bitcast.21), channel_id=1, replica_groups=mesh['row'=8,'col'=64] {'col'}, dimensions={0} | all-to-all | bytes 1048576 | tf_op jit(solution)/shard_map/all_to_all | solution.py:329
  106.0 0.8 copy.15
  (1 shorter events, 0.0 us)
Async XLA Ops:
  23.6 16.8 %copy-start = (bf16[32,4096]{1,0:T(8,128)(2,1)S(1)}, bf16[32,4096]{1,0:T(8,128)(2,1)}, u32[]{:S(2)}) copy-start(bf16[32,4096]{1,0:T(8,128)(2,1)} %x_ref.3) | copy-start | bytes 786436
  23.6 16.7 %copy-start.1 = (bf16[32,2048]{1,0:T(8,128)(2,1)S(1)}, bf16[32,2048]{1,0:T(8,128)(2,1)}, u32[]{:S(2)}) copy-start(bf16[32,2048]{1,0:T(8,128)(2,1)} %y_ref.3) | copy-start | bytes 393220
  40.3 0.7 copy-start.2

commit v4 on v3

--- a/solution.py
+++ b/solution.py
@@ -12,7 +12,7 @@
 LANES = 128
 DIM = 32
 DEPTH = 112
-PACK = 18
+PACK = 17
 VMEM_LIMIT = 16 * 2**20
 
 epsilon = 0.01
@@ -182,7 +182,8 @@
         out_ref[c * rows : (c + 1) * rows, :] = value
 
 
-def tgt_kernel(parts, copies, log_rows, slots, count, in_ref, x_ref, y_ref, f_ref, out_ref, xa, ya, top_ref, total_ref):
+def tgt_kernel(parts, copies, log_rows, count, slots_in, in_ref, x_ref, y_ref, f_out, out_ref, slots, f_ref, sems, xa, ya, top_ref, total_ref):
+    fetched = fetch((slots_in,), (slots,), sems)[0]
     fill_src(x_ref, xa)
     fill_tgt(y_ref, ya)
     for b in range(ya.shape[0]):
@@ -198,7 +199,10 @@
             one = bias[row : row + 1, :]
             xa[b, 3 * DIM : DEPTH, lanes] = bias_rows(one)
             f_ref[row : row + 1, :] = unit * one + square[:, lanes] * (1.0 / DIM)
+    written = pltpu.make_async_copy(f_ref, f_out, sems.at[1])
     clear(top_ref, total_ref)
+    fetched.wait()
+    written.start()
 
     lse_tiles(
         count[0, 0],
@@ -211,9 +215,11 @@
         total_ref,
     )
     spread_rows(ya.shape[0], top_ref, total_ref, out_ref, copies)
-
-
-def bary_kernel(parts, log_cols, slots, count, in_ref, x_ref, y_ref, g_ref, out_ref, xa, ya, yb, top_ref, acc_ref):
+    written.wait()
+
+
+def bary_kernel(parts, log_cols, count, slots_in, in_ref, x_ref, y_ref, g_out, out_ref, slots, g_ref, sems, xa, ya, yb, top_ref, acc_ref):
+    fetched = fetch((slots_in,), (slots,), sems)[0]
     fill_src(x_ref, xa)
     fill_tgt(y_ref, ya)
     for b in range(xa.shape[0]):
@@ -233,9 +239,12 @@
             one = bias[row : row + 1, :]
             ya[b, 3 * DIM : DEPTH, lanes] = bias_rows(one)
             g_ref[row : row + 1, :] = unit * one + square[:, lanes] * (1.0 / DIM)
+    written = pltpu.make_async_copy(g_ref, g_out, sems.at[1])
     top_ref[...] = jnp.full(top_ref.shape, very_low, F32)
     acc_ref[...] = jnp.zeros(acc_ref.shape, F32)
 
+    fetched.wait()
+    written.start()
     spare = xa.shape[0]
 
     def step(q, carry):
@@ -268,39 +277,55 @@
         live = total > 0.0
         lse = jnp.where(live, top_ref[b] + jnp.log2(total), very_low)
         mean = acc_ref[b, 0:32, :] * jnp.where(live, 1.0 / total, 0.0)
-        for h in range(DIM // 8):
-            for k in range(per):
-                lanes = slice(k * LANES, (k + 1) * LANES)
-                owner = (h * spare * per + b * per + k) // 2
-                at = owner * PACK + k % 2 * 8
-                out_ref[at : at + 8, :] = mean[h * 8 : h * 8 + 8, lanes]
-                at = owner * PACK + 16 + k % 2
-                out_ref[at : at + 1, :] = lse[:, lanes]
-
+        for k in range(per):
+            lanes = slice(k * LANES, (k + 1) * LANES)
+            for h in range(2):
+                at = ((b * per + k) * 2 + h) * PACK
+                out_ref[at : at + 16, :] = mean[h * 16 : h * 16 + 16, lanes]
+                out_ref[at + 16 : at + 17, :] = lse[:, lanes]
+    written.wait()
 
 def mean_kernel(parts, in_ref, out_ref):
-    for half in range(2):
-        logs = [in_ref[c * PACK + 16 + half : c * PACK + 17 + half, :] for c in range(parts)]
-        top = functools.reduce(jnp.maximum, logs)
-        total = jnp.zeros_like(top)
-        value = jnp.zeros((8, LANES), F32)
-        for c in range(parts):
-            weight = jnp.exp2(logs[c] - top)
-            total = total + weight
-            at = c * PACK + half * 8
-            value = value + weight * in_ref[at : at + 8, :]
-        value = value / total
-        for c in range(parts):
-            at = c * 16 + half * 8
-            out_ref[at : at + 8, :] = value
+    logs = [in_ref[c * PACK + 16 : c * PACK + 17, :] for c in range(parts)]
+    top = functools.reduce(jnp.maximum, logs)
+    total = jnp.zeros_like(top)
+    value = jnp.zeros((16, LANES), F32)
+    for c in range(parts):
+        weight = jnp.exp2(logs[c] - top)
+        total = total + weight
+        value = value + weight * in_ref[c * PACK : c * PACK + 16, :]
+    value = value / total
+    for c in range(parts):
+        out_ref[c * 16 : (c + 1) * 16, :] = value
+
+
+def place_kernel(in_ref, out_ref, sems):
+    half = in_ref.shape[0] // 2
+    copies = []
+    for d in range(4):
+        for k in range(2):
+            runs = pl.ds(k * half, half)
+            copies.append(
+                pltpu.make_async_copy(
+                    in_ref.at[runs, d // 2, d % 2], out_ref.at[d, runs], sems.at[2 * d + k]
+                )
+            )
+    for copy in copies:
+        copy.start()
+    for copy in copies:
+        copy.wait()
 
 
 def whole(count):
     return [pl.BlockSpec(memory_space=pltpu.VMEM)] * count
 
 
-def scalars():
-    return [pl.BlockSpec(memory_space=pltpu.SMEM)] * 2
+def scalar():
+    return pl.BlockSpec(memory_space=pltpu.SMEM)
+
+
+def far():
+    return pl.BlockSpec(memory_space=pltpu.HBM)
 
 
 def body(src_latent, tgt_latent, g_start, pairs, counts):
@@ -311,7 +336,7 @@
     other = n_col // side
     groups_z = [[z * side + y for z in range(other)] for y in range(side)]
     groups_y = [[z * side + y for y in range(side)] for z in range(other)]
-    slots = pairs.reshape(pairs.shape[2:]).T
+    slots = pltpu.with_memory_space_constraint(pairs.reshape(pairs.shape[2:]).T, pltpu.HBM)
     count = counts
     s_blocks, t_blocks = src_len // BLOCK, tgt_len // BLOCK
     s_rows, t_rows = src_len // LANES, tgt_len // LANES
@@ -323,6 +348,13 @@
 
     def line(blocks, rows=8):
         return pltpu.VMEM((blocks, rows, BLOCK), F32)
+
+    def side_refs(rows):
+        return (
+            pltpu.SMEM(slots.shape, jnp.int32),
+            pltpu.VMEM((rows, LANES), F32),
+            pltpu.SemaphoreType.DMA((2,)),
+        )
 
     def exchange(x, axis, parts, groups=None):
         width = x.shape[0] // parts * LANES
@@ -337,7 +369,7 @@
     lse = pl.pallas_call(
         functools.partial(src_kernel, other),
         out_shape=rows_of(other * s_rows),
-        in_specs=scalars()[:1] + [pl.BlockSpec(memory_space=pltpu.HBM)] * 4,
+        in_specs=[scalar()] + [far()] * 4,
         out_specs=whole(1)[0],
         scratch_shapes=[
             pltpu.SMEM(slots.shape, jnp.int32),
@@ -348,9 +380,9 @@
             aug(s_blocks), aug(t_blocks), line(s_blocks + 1), line(s_blocks + 1)],
         compiler_params=pltpu.CompilerParams(vmem_limit_bytes=VMEM_LIMIT),
         name="src_pass",
-    )(count, *[
+    )(count, slots, *[
         pltpu.with_memory_space_constraint(a, pltpu.HBM)
-        for a in (slots, src_latent, tgt_latent, g_start.reshape(1, -1))
+        for a in (src_latent, tgt_latent, g_start.reshape(1, -1))
     ])
     lse = exchange(lse, "col", other, groups_z)
     lse = pl.pallas_call(
@@ -365,19 +397,20 @@
     f_new, lse = pl.pallas_call(
         functools.partial(tgt_kernel, side, n_row, log_rows),
         out_shape=(rows_of(s_rows), rows_of(n_row * t_rows)),
-        in_specs=scalars() + whole(3),
-        out_specs=tuple(whole(2)),
-        scratch_shapes=[aug(s_blocks), aug(t_blocks), line(t_blocks + 1), line(t_blocks + 1)],
+        in_specs=[scalar(), far()] + whole(3),
+        out_specs=(far(), whole(1)[0]),
+        scratch_shapes=[*side_refs(s_rows), aug(s_blocks), aug(t_blocks), line(t_blocks + 1), line(t_blocks + 1)],
         compiler_params=pltpu.CompilerParams(vmem_limit_bytes=VMEM_LIMIT),
         name="tgt_pass",
-    )(slots, count, lse, src_latent, tgt_latent)
+    )(count, slots, lse, src_latent, tgt_latent)
     lse = exchange(lse, "row", n_row)
     g_new, means = pl.pallas_call(
         functools.partial(bary_kernel, n_row, log_cols),
         out_shape=(rows_of(t_rows), rows_of(n_col * PACK)),
-        in_specs=scalars() + whole(3),
-        out_specs=tuple(whole(2)),
+        in_specs=[scalar(), far()] + whole(3),
+        out_specs=(far(), whole(1)[0]),
         scratch_shapes=[
+            *side_refs(t_rows),
             aug(s_blocks),
             aug(t_blocks),
             pltpu.VMEM((t_blocks, 48, BLOCK), BF16),
@@ -386,7 +419,7 @@
         ],
         compiler_params=pltpu.CompilerParams(vmem_limit_bytes=VMEM_LIMIT),
         name="bary_pass",
-    )(slots, count, lse, src_latent, tgt_latent)
+    )(count, slots, lse, src_latent, tgt_latent)
     means = exchange(means, "col", n_col)
     means = pl.pallas_call(
         functools.partial(mean_kernel, n_col),
@@ -397,7 +430,15 @@
         name="bary_merge",
     )(means)
     means = exchange(means, "col", n_col)
-    tiles = means.reshape(DIM // 8, s_rows, 8, LANES)
+    tiles = pl.pallas_call(
+        place_kernel,
+        out_shape=jax.ShapeDtypeStruct((DIM // 8, s_rows, 8, LANES), F32),
+        in_specs=whole(1),
+        out_specs=far(),
+        scratch_shapes=[pltpu.SemaphoreType.DMA((8,))],
+        compiler_params=pltpu.CompilerParams(vmem_limit_bytes=VMEM_LIMIT),
+        name="bary_place",
+    )(means.reshape(s_rows, 2, 2, 8, LANES))
     bary = tiles.transpose(0, 2, 1, 3).reshape(DIM, src_len)
     return f_new.reshape(-1), g_new.reshape(-1), bary
 

time: 108 us -> 105 us (0.972)
  the two profiles are of different devices: /device:TPU:2 before, /device:TPU:8 now
where the time goes in v4:
time: 105 us
  blocking collectives  97.2 us (93%)
  Pallas kernels  6.11 us (6%)
  between operations  1.32 us (1%)
    all_to_all x5, blocking collectives, exchange(): lax.all_to_all(x.reshape(parts, width), axis, 0, 0, axis_index_groups=gro...  97.2 us

profile of v4, /device:TPU:8, one launch (start us, length us, event | category | flops | bytes accessed | tf_op | source)
XLA Modules:
  0.0 104.6 jit_solution(1145593721254168636)
XLA Ops:
  1.3 2.0 %src_pass.1 = f32[256,128]{1,0:T(8,128)S(1)} custom-call(s32[1,1]{1,0:T(1,128)S(6)} %copy.13.count, s32[2,8]{1,0:T(2,128)} %bitcast.30, bf16[32,4096]{1,0:T(8,128)(2,1)} %x_ref.3, bf16[32,2048]{1,0:T(8,128)(2,1)} %y_ref.3, f32[1,2048]{1,0:T(1,128)} %bitcast.33), custom_call_target="tpu_custom_call" | custom-call | tf_op jit(solution)/shard_map/src_pass/pallas_call | solution.py:369
  3.3 20.9 %all_to_all.45 = f32[8,1,4096]{2,1,0:T(1,128)S(1)} all-to-all(f32[8,1,4096]{2,1,0:T(1,128)S(1)} %bitcast.24), channel_id=1, replica_groups={{0,8,16,24,32,40,48,56},{1,9,17,25,33,41,49,57},{2,10,18,26,34,42,50,58..., dimensions={0} | all-to-all | bytes 262144 | tf_op jit(solution)/shard_map/all_to_all | solution.py:361
  24.2 0.0 copy-start
  24.2 0.0 copy-start.1
  24.2 14.5 %all_to_all.46 = f32[8,1,4096]{2,1,0:T(1,128)S(1)} all-to-all(f32[8,1,4096]{2,1,0:T(1,128)S(1)} %bitcast.26), channel_id=1, replica_groups={{0,1,2,3,4,5,6,7},{8,9,10,11,12,13,14,15},{16,17,18,19,20,21,22,23},{24..., dimensions={0} | all-to-all | bytes 262144 | tf_op jit(solution)/shard_map/all_to_all | solution.py:361
  38.7 0.0 copy-done
  38.7 0.0 copy-done.1
  38.8 1.4 %tgt_pass.1 = (f32[32,128]{1,0:T(8,128)}, f32[128,128]{1,0:T(8,128)S(1)}) custom-call(s32[1,1]{1,0:T(1,128)S(6)} %copy.13.count, s32[2,8]{1,0:T(2,128)} %bitcast.31, f32[256,128]{1,0:T(8,128)S(1)} %bitcast.23, bf16[32,4096]{1,0:T(8,128)(2,1)S(1)} %copy-done, bf16[32,2048]{1,0:T(8,128)(2,1)S(1)} %copy-done.1), custom_call_target="tpu_custom_call" | custom-call | tf_op jit(solution)/shard_map/tgt_pass/pallas_call | solution.py:397
  40.1 11.4 %all_to_all.47 = f32[8,1,2048]{2,1,0:T(1,128)S(1)} all-to-all(f32[8,1,2048]{2,1,0:T(1,128)S(1)} %bitcast.28), channel_id=1, replica_groups=mesh['row'=8,'col'=64] {'row'}, dimensions={0} | all-to-all | bytes 131072 | tf_op jit(solution)/shard_map/all_to_all | solution.py:361
  51.6 1.7 %bary_pass.1 = (f32[16,128]{1,0:T(8,128)}, f32[1088,128]{1,0:T(8,128)S(1)}) custom-call(s32[1,1]{1,0:T(1,128)S(6)} %copy.13.count, s32[2,8]{1,0:T(2,128)} %bitcast.32, f32[128,128]{1,0:T(8,128)S(1)} %bitcast.27, bf16[32,4096]{1,0:T(8,128)(2,1)S(1)} %copy-done, bf16[32,2048]{1,0:T(8,128)(2,1)S(1)} %copy-done.1), custom_call_target="tpu_custom_call" | custom-call | tf_op jit(solution)/shard_map/bary_pass/pallas_call | solution.py:407
  53.3 26.6 %all_to_all.48 = f32[64,1,2176]{2,1,0:T(1,128)S(1)} all-to-all(f32[64,1,2176]{2,1,0:T(1,128)S(1)} %bitcast.22), channel_id=1, replica_groups=mesh['row'=8,'col'=64] {'col'}, dimensions={0} | all-to-all | bytes 1114112 | tf_op jit(solution)/shard_map/all_to_all | solution.py:361
  79.9 0.2 bary_merge.1
  80.1 23.7 %all_to_all.49 = f32[64,1,2048]{2,1,0:T(1,128)S(1)} all-to-all(f32[64,1,2048]{2,1,0:T(1,128)S(1)} %bitcast.20), channel_id=1, replica_groups=mesh['row'=8,'col'=64] {'col'}, dimensions={0} | all-to-all | bytes 1048576 | tf_op jit(solution)/shard_map/all_to_all | solution.py:361
  103.8 0.8 bary_place.1
  (1 shorter events, 0.0 us)
Async XLA Ops:
  24.2 14.6 %copy-start = (bf16[32,4096]{1,0:T(8,128)(2,1)S(1)}, bf16[32,4096]{1,0:T(8,128)(2,1)}, u32[]{:S(2)}) copy-start(bf16[32,4096]{1,0:T(8,128)(2,1)} %x_ref.3) | copy-start | bytes 786436
  24.2 14.5 %copy-start.1 = (bf16[32,2048]{1,0:T(8,128)(2,1)S(1)}, bf16[32,2048]{1,0:T(8,128)(2,1)}, u32[]{:S(2)}) copy-start(bf16[32,2048]{1,0:T(8,128)(2,1)} %y_ref.3) | copy-start | bytes 393220

commit v5 on v4

--- a/solution.py
+++ b/solution.py
@@ -44,18 +44,24 @@
     return jnp.where(row < 3, 1.0, 0.0).astype(BF16)
 
 
-def fill_src(x_ref, xa):
-    for b in range(xa.shape[0]):
+def fill_src(x_ref, xs_ref):
+    for b in range(xs_ref.shape[0]):
         xs = x_ref[:, b * BLOCK : (b + 1) * BLOCK].astype(F32) * cross_scale
         for k, piece in enumerate(pieces(xs)):
-            xa[b, k * DIM : (k + 1) * DIM, :] = piece.astype(BF16)
-
-
-def fill_tgt(y_ref, ya):
-    for b in range(ya.shape[0]):
-        ys = y_ref[:, b * BLOCK : (b + 1) * BLOCK]
-        for k in range(3):
-            ya[b, k * DIM : (k + 1) * DIM, :] = ys
+            xs_ref[b, k * DIM : (k + 1) * DIM, :] = piece.astype(BF16)
+
+
+def src_operand(xs_ref, s, tail):
+    return jnp.concatenate([xs_ref[s], tail], axis=0)
+
+
+def tgt_block(y_ref, t):
+    return y_ref[:, pl.ds(pl.multiple_of(t * BLOCK, BLOCK), BLOCK)]
+
+
+def tgt_operand(y_ref, t, tail):
+    block = tgt_block(y_ref, t)
+    return jnp.concatenate([block, block, block, tail], axis=0)
 
 
 def tile_scores(left, right):
@@ -65,7 +71,8 @@
 CHUNK = 128
 
 
-UNROLL = 2
+UNROLL = 4
+BARY_UNROLL = 2
 
 
 def tile_lse(left, right):
@@ -145,34 +152,32 @@
     return copies
 
 
-def src_kernel(parts, count, slots_in, x_in, y_in, g_in, out_ref, slots, x_ref, y_ref, g_ref, sems, xa, ya, top_ref, total_ref):
+def src_kernel(parts, count, slots_in, x_in, y_in, g_in, out_ref, xs_ref, slots, x_ref, y_ref, g_ref, sems, bias_ref, top_ref, total_ref):
     copies = fetch(
         (x_in, y_in, g_in, slots_in), (x_ref, y_ref, g_ref, slots), sems
     )
-    for b in range(xa.shape[0]):
-        xa[b, 3 * DIM : DEPTH, :] = one_rows(BLOCK)
     clear(top_ref, total_ref)
     for copy in copies:
         copy.wait()
-    fill_src(x_ref, xa)
-    fill_tgt(y_ref, ya)
-    for b in range(ya.shape[0]):
+    fill_src(x_ref, xs_ref)
+    for b in range(bias_ref.shape[0]):
         ys = y_ref[:, b * BLOCK : (b + 1) * BLOCK].astype(F32)
         square = jnp.sum(ys * ys, axis=0, keepdims=True)
         start = g_ref[:, b * BLOCK : (b + 1) * BLOCK]
-        ya[b, 3 * DIM : DEPTH, :] = bias_rows(start / unit - square * square_scale)
-
+        bias_ref[b] = bias_rows(start / unit - square * square_scale)
+    ones = one_rows(BLOCK)
+    blocks = xs_ref.shape[0]
     lse_tiles(
         count[0, 0],
         slots,
-        lambda s, t: ya[t],
-        lambda s, t: xa[s],
+        lambda s, t: tgt_operand(y_ref, t, bias_ref[t]),
+        lambda s, t: src_operand(xs_ref, s, ones),
         lambda s, t: s,
-        xa.shape[0],
+        blocks,
         top_ref,
         total_ref,
     )
-    spread_rows(xa.shape[0], top_ref, total_ref, out_ref, parts)
+    spread_rows(blocks, top_ref, total_ref, out_ref, parts)
 
 
 def merge_kernel(parts, in_ref, out_ref):
@@ -182,86 +187,78 @@
         out_ref[c * rows : (c + 1) * rows, :] = value
 
 
-def tgt_kernel(parts, copies, log_rows, count, slots_in, in_ref, x_ref, y_ref, f_out, out_ref, slots, f_ref, sems, xa, ya, top_ref, total_ref):
+def tgt_kernel(parts, copies, log_rows, count, slots_in, in_ref, xs_ref, x_ref, y_ref, f_out, out_ref, slots, f_ref, sems, bias_ref, top_ref, total_ref):
     fetched = fetch((slots_in,), (slots,), sems)[0]
-    fill_src(x_ref, xa)
-    fill_tgt(y_ref, ya)
-    for b in range(ya.shape[0]):
-        ya[b, 3 * DIM : DEPTH, :] = one_rows(BLOCK)
+    clear(top_ref, total_ref)
     bias = -log_rows - merged(in_ref, parts)
     per = BLOCK // LANES
-    for b in range(xa.shape[0]):
+    for b in range(bias_ref.shape[0]):
         xs = x_ref[:, b * BLOCK : (b + 1) * BLOCK].astype(F32)
         square = jnp.sum(xs * xs, axis=0, keepdims=True)
         for k in range(per):
             row = b * per + k
             lanes = slice(k * LANES, (k + 1) * LANES)
             one = bias[row : row + 1, :]
-            xa[b, 3 * DIM : DEPTH, lanes] = bias_rows(one)
+            bias_ref[b, :, lanes] = bias_rows(one)
             f_ref[row : row + 1, :] = unit * one + square[:, lanes] * (1.0 / DIM)
     written = pltpu.make_async_copy(f_ref, f_out, sems.at[1])
-    clear(top_ref, total_ref)
     fetched.wait()
     written.start()
-
+    ones = one_rows(BLOCK)
+    blocks = y_ref.shape[1] // BLOCK
     lse_tiles(
         count[0, 0],
         slots,
-        lambda s, t: xa[s],
-        lambda s, t: ya[t],
+        lambda s, t: src_operand(xs_ref, s, bias_ref[s]),
+        lambda s, t: tgt_operand(y_ref, t, ones),
         lambda s, t: t,
-        ya.shape[0],
+        blocks,
         top_ref,
         total_ref,
     )
-    spread_rows(ya.shape[0], top_ref, total_ref, out_ref, copies)
+    spread_rows(blocks, top_ref, total_ref, out_ref, copies)
     written.wait()
 
 
-def bary_kernel(parts, log_cols, count, slots_in, in_ref, x_ref, y_ref, g_out, out_ref, slots, g_ref, sems, xa, ya, yb, top_ref, acc_ref):
+def bary_kernel(parts, log_cols, count, slots_in, in_ref, xs_ref, y_ref, g_out, out_ref, slots, g_ref, sems, bias_ref, top_ref, acc_ref):
     fetched = fetch((slots_in,), (slots,), sems)[0]
-    fill_src(x_ref, xa)
-    fill_tgt(y_ref, ya)
-    for b in range(xa.shape[0]):
-        xa[b, 3 * DIM : DEPTH, :] = one_rows(BLOCK)
+    top_ref[...] = jnp.full(top_ref.shape, very_low, F32)
+    acc_ref[...] = jnp.zeros(acc_ref.shape, F32)
     bias = -log_cols - merged(in_ref, parts)
     per = BLOCK // LANES
-    first_row = lax.broadcasted_iota(jnp.int32, (16, BLOCK), 0) == 0
-    for b in range(ya.shape[0]):
-        y_block = y_ref[:, b * BLOCK : (b + 1) * BLOCK]
-        ys = y_block.astype(F32)
+    for b in range(bias_ref.shape[0]):
+        ys = y_ref[:, b * BLOCK : (b + 1) * BLOCK].astype(F32)
         square = jnp.sum(ys * ys, axis=0, keepdims=True)
-        yb[b, 0:32, :] = y_block
-        yb[b, 32:48, :] = jnp.where(first_row, 1.0, 0.0).astype(BF16)
         for k in range(per):
             row = b * per + k
             lanes = slice(k * LANES, (k + 1) * LANES)
             one = bias[row : row + 1, :]
-            ya[b, 3 * DIM : DEPTH, lanes] = bias_rows(one)
+            bias_ref[b, :, lanes] = bias_rows(one)
             g_ref[row : row + 1, :] = unit * one + square[:, lanes] * (1.0 / DIM)
     written = pltpu.make_async_copy(g_ref, g_out, sems.at[1])
-    top_ref[...] = jnp.full(top_ref.shape, very_low, F32)
-    acc_ref[...] = jnp.zeros(acc_ref.shape, F32)
-
     fetched.wait()
     written.start()
-    spare = xa.shape[0]
+    spare = xs_ref.shape[0]
+    ones = one_rows(BLOCK)
+    first_row = lax.broadcasted_iota(jnp.int32, (16, BLOCK), 0) == 0
+    total_row = jnp.where(first_row, 1.0, 0.0).astype(BF16)
 
     def step(q, carry):
         tiles = []
-        for u in range(2):
-            p = q * 2 + u
+        for u in range(BARY_UNROLL):
+            p = q * BARY_UNROLL + u
             live = p < count[0, 0]
             p = jnp.minimum(p, count[0, 0] - 1)
             s, t = slots[0, p], slots[1, p]
-            scores = tile_scores(ya[t], xa[s])
+            scores = tile_scores(tgt_operand(y_ref, t, bias_ref[t]), src_operand(xs_ref, s, ones))
+            values = jnp.concatenate([tgt_block(y_ref, t), total_row], axis=0)
             top = part = None
-            for c in range(0, BLOCK, 128):
-                score = scores[c : c + 128, :]
+            for c in range(0, BLOCK, CHUNK):
+                score = scores[c : c + CHUNK, :]
                 most = jnp.max(score, axis=0, keepdims=True)
                 old, top = top, most if c == 0 else jnp.maximum(top, most)
                 weight = jnp.exp2(score - top).astype(BF16)
-                more = jnp.dot(yb[t, :, c : c + 128], weight, preferred_element_type=F32)
+                more = jnp.dot(values[:, c : c + CHUNK], weight, preferred_element_type=F32)
                 part = more if c == 0 else part * jnp.exp2(old - top) + more
             tiles.append((top, part, jnp.where(live, s, spare)))
         for top, part, at in tiles:
@@ -271,7 +268,7 @@
             top_ref[at] = most
         return carry
 
-    lax.fori_loop(0, lax.div(count[0, 0] + 2 - 1, 2), step, 0)
+    lax.fori_loop(0, lax.div(count[0, 0] + BARY_UNROLL - 1, BARY_UNROLL), step, 0)
     for b in range(spare):
         total = acc_ref[b, 32:33, :]
         live = total > 0.0
@@ -343,8 +340,8 @@
     log_rows = math.log2(src_len * n_row)
     log_cols = math.log2(tgt_len * n_col)
 
-    def aug(blocks):
-        return pltpu.VMEM((blocks, DEPTH, BLOCK), BF16)
+    def tails(blocks):
+        return pltpu.VMEM((blocks, 16, BLOCK), BF16)
 
     def line(blocks, rows=8):
         return pltpu.VMEM((blocks, rows, BLOCK), F32)
@@ -366,18 +363,21 @@
     def rows_of(n):
         return jax.ShapeDtypeStruct((n, LANES), F32)
 
-    lse = pl.pallas_call(
+    lse, xs = pl.pallas_call(
         functools.partial(src_kernel, other),
-        out_shape=rows_of(other * s_rows),
+        out_shape=(
+            rows_of(other * s_rows),
+            jax.ShapeDtypeStruct((s_blocks, 3 * DIM, BLOCK), BF16),
+        ),
         in_specs=[scalar()] + [far()] * 4,
-        out_specs=whole(1)[0],
+        out_specs=tuple(whole(2)),
         scratch_shapes=[
             pltpu.SMEM(slots.shape, jnp.int32),
             pltpu.VMEM(src_latent.shape, BF16),
             pltpu.VMEM(tgt_latent.shape, BF16),
             pltpu.VMEM((1, tgt_len), F32),
             pltpu.SemaphoreType.DMA((4,)),
-            aug(s_blocks), aug(t_blocks), line(s_blocks + 1), line(s_blocks + 1)],
+            tails(t_blocks), line(s_blocks + 1), line(s_blocks + 1)],
         compiler_params=pltpu.CompilerParams(vmem_limit_bytes=VMEM_LIMIT),
         name="src_pass",
     )(count, slots, *[
@@ -397,12 +397,12 @@
     f_new, lse = pl.pallas_call(
         functools.partial(tgt_kernel, side, n_row, log_rows),
         out_shape=(rows_of(s_rows), rows_of(n_row * t_rows)),
-        in_specs=[scalar(), far()] + whole(3),
+        in_specs=[scalar(), far()] + whole(4),
         out_specs=(far(), whole(1)[0]),
-        scratch_shapes=[*side_refs(s_rows), aug(s_blocks), aug(t_blocks), line(t_blocks + 1), line(t_blocks + 1)],
+        scratch_shapes=[*side_refs(s_rows), tails(s_blocks), line(t_blocks + 1), line(t_blocks + 1)],
         compiler_params=pltpu.CompilerParams(vmem_limit_bytes=VMEM_LIMIT),
         name="tgt_pass",
-    )(count, slots, lse, src_latent, tgt_latent)
+    )(count, slots, lse, xs, src_latent, tgt_latent)
     lse = exchange(lse, "row", n_row)
     g_new, means = pl.pallas_call(
         functools.partial(bary_kernel, n_row, log_cols),
@@ -411,15 +411,13 @@
         out_specs=(far(), whole(1)[0]),
         scratch_shapes=[
             *side_refs(t_rows),
-            aug(s_blocks),
-            aug(t_blocks),
-            pltpu.VMEM((t_blocks, 48, BLOCK), BF16),
+            tails(t_blocks),
             line(s_blocks + 1, 1),
             pltpu.VMEM((s_blocks + 1, 48, BLOCK), F32),
         ],
         compiler_params=pltpu.CompilerParams(vmem_limit_bytes=VMEM_LIMIT),
         name="bary_pass",
-    )(count, slots, lse, src_latent, tgt_latent)
+    )(count, slots, lse, xs, tgt_latent)
     means = exchange(means, "col", n_col)
     means = pl.pallas_call(
         functools.partial(mean_kernel, n_col),

time: 105 us -> 105 us (level)
  blocking collectives: 97.2 us -> 96 us
    all_to_all x5, blocking collectives: 97.2 us -> 96 us  [exchange(): lax.all_to_all(x.reshape(parts, width), axis, 0, 0, axis_index_groups=gro...]
where the time goes in v5:
time: 105 us; the launch traced here: 104 us
  blocking collectives  96 us (91%)
  Pallas kernels  6.86 us (7%)
  between operations  1.32 us (1%)
    all_to_all x5, blocking collectives, exchange(): lax.all_to_all(x.reshape(parts, width), axis, 0, 0, axis_index_groups=gro...  96 us
    pallas_call x1, Pallas kernels, body(): pl.pallas_call(functools.partial(src_kernel, other), out_shape=(rows_of(o...  2.34 us

profile of v5, /device:TPU:8, one launch (start us, length us, event | category | flops | bytes accessed | tf_op | source)
XLA Modules:
  0.0 104.2 jit_solution(8248424673562958360)
XLA Ops:
  1.3 2.3 %src_pass.1 = (f32[256,128]{1,0:T(8,128)S(1)}, bf16[8,96,512]{2,1,0:T(8,128)(2,1)S(1)}) custom-call(s32[1,1]{1,0:T(1,128)S(6)} %copy.13.count, s32[2,8]{1,0:T(2,128)} %bitcast.30, bf16[32,4096]{1,0:T(8,128)(2,1)} %x_ref.1, bf16[32,2048]{1,0:T(8,128)(2,1)} %y_ref.3, f32[1,2048]{1,0:T(1,128)} %bitcast.33), custom_call_target="tpu_custom_call" | custom-call | tf_op jit(solution)/shard_map/src_pass/pallas_call | solution.py:366
  3.6 20.1 %all_to_all.45 = f32[8,1,4096]{2,1,0:T(1,128)S(1)} all-to-all(f32[8,1,4096]{2,1,0:T(1,128)S(1)} %bitcast.27), channel_id=1, replica_groups={{0,8,16,24,32,40,48,56},{1,9,17,25,33,41,49,57},{2,10,18,26,34,42,50,58..., dimensions={0} | all-to-all | bytes 262144 | tf_op jit(solution)/shard_map/all_to_all | solution.py:358
  23.8 0.0 copy-start.1
  23.8 0.0 copy-start
  23.8 15.1 %all_to_all.46 = f32[8,1,4096]{2,1,0:T(1,128)S(1)} all-to-all(f32[8,1,4096]{2,1,0:T(1,128)S(1)} %bitcast.24), channel_id=1, replica_groups={{0,1,2,3,4,5,6,7},{8,9,10,11,12,13,14,15},{16,17,18,19,20,21,22,23},{24..., dimensions={0} | all-to-all | bytes 262144 | tf_op jit(solution)/shard_map/all_to_all | solution.py:358
  39.0 0.0 copy-done.1
  39.0 0.0 copy-done
  39.0 1.7 %tgt_pass.1 = (f32[32,128]{1,0:T(8,128)}, f32[128,128]{1,0:T(8,128)S(1)}) custom-call(s32[1,1]{1,0:T(1,128)S(6)} %copy.13.count, s32[2,8]{1,0:T(2,128)} %bitcast.31, f32[256,128]{1,0:T(8,128)S(1)} %bitcast.25, bf16[8,96,512]{2,1,0:T(8,128)(2,1)S(1)} %get-tuple-element.10.xs_ref, bf16[32,4096]{1,0:T(8,128)(2,1)S(1)} %copy-done.1, bf16[32,2048]{1,0:T(8,128)(2,1)S(1)} %copy-done), custom_call_target="tpu_custom_call" | custom-call | tf_op jit(solution)/shard_map/tgt_pass/pallas_call | solution.py:397
  40.7 10.7 %all_to_all.47 = f32[8,1,2048]{2,1,0:T(1,128)S(1)} all-to-all(f32[8,1,2048]{2,1,0:T(1,128)S(1)} %bitcast.28), channel_id=1, replica_groups=mesh['row'=8,'col'=64] {'row'}, dimensions={0} | all-to-all | bytes 131072 | tf_op jit(solution)/shard_map/all_to_all | solution.py:358
  51.4 1.7 %bary_pass.1 = (f32[16,128]{1,0:T(8,128)}, f32[1088,128]{1,0:T(8,128)S(1)}) custom-call(s32[1,1]{1,0:T(1,128)S(6)} %copy.13.count, s32[2,8]{1,0:T(2,128)} %bitcast.32, f32[128,128]{1,0:T(8,128)S(1)} %bitcast.26, bf16[8,96,512]{2,1,0:T(8,128)(2,1)S(1)} %get-tuple-element.10.xs_ref, bf16[32,2048]{1,0:T(8,128)(2,1)S(1)} %copy-done), custom_call_target="tpu_custom_call" | custom-call | tf_op jit(solution)/shard_map/bary_pass/pallas_call | solution.py:407
  53.1 26.4 %all_to_all.48 = f32[64,1,2176]{2,1,0:T(1,128)S(1)} all-to-all(f32[64,1,2176]{2,1,0:T(1,128)S(1)} %bitcast.22), channel_id=1, replica_groups=mesh['row'=8,'col'=64] {'col'}, dimensions={0} | all-to-all | bytes 1114112 | tf_op jit(solution)/shard_map/all_to_all | solution.py:358
  79.5 0.2 bary_merge.1
  79.7 23.7 %all_to_all.49 = f32[64,1,2048]{2,1,0:T(1,128)S(1)} all-to-all(f32[64,1,2048]{2,1,0:T(1,128)S(1)} %bitcast.20), channel_id=1, replica_groups=mesh['row'=8,'col'=64] {'col'}, dimensions={0} | all-to-all | bytes 1048576 | tf_op jit(solution)/shard_map/all_to_all | solution.py:358
  103.4 0.8 bary_place.1
  (1 shorter events, 0.0 us)
Async XLA Ops:
  23.8 15.2 %copy-start.1 = (bf16[32,4096]{1,0:T(8,128)(2,1)S(1)}, bf16[32,4096]{1,0:T(8,128)(2,1)}, u32[]{:S(2)}) copy-start(bf16[32,4096]{1,0:T(8,128)(2,1)} %x_ref.1) | copy-start | bytes 786436
  23.8 15.1 %copy-start = (bf16[32,2048]{1,0:T(8,128)(2,1)S(1)}, bf16[32,2048]{1,0:T(8,128)(2,1)}, u32[]{:S(2)}) copy-start(bf16[32,2048]{1,0:T(8,128)(2,1)} %y_ref.3) | copy-start | bytes 393220

commit v6 on v5

--- a/solution.py
+++ b/solution.py
@@ -13,6 +13,8 @@
 DIM = 32
 DEPTH = 112
 PACK = 17
+LATE = 0
+HOLD = 5000
 VMEM_LIMIT = 16 * 2**20
 
 epsilon = 0.01
@@ -238,6 +240,11 @@
     written = pltpu.make_async_copy(g_ref, g_out, sems.at[1])
     fetched.wait()
     written.start()
+
+    @pl.when(lax.rem(lax.axis_index("row"), 2) == LATE)
+    def _():
+        pl.delay(HOLD)
+
     spare = xs_ref.shape[0]
     ones = one_rows(BLOCK)
     first_row = lax.broadcasted_iota(jnp.int32, (16, BLOCK), 0) == 0

time: 105 us -> 102 us (0.971)
  blocking collectives: 96 us -> 88.4 us
  Pallas kernels: 6.86 us -> 11.9 us
    all_to_all x5, blocking collectives: 96 us -> 88.4 us  [exchange(): lax.all_to_all(x.reshape(parts, width), axis, 0, 0, axis_index_groups=gro...]
    pallas_call x1, Pallas kernels: 1.71 us -> 6.71 us  [body(): pl.pallas_call(functools.partial(bary_kernel, n_row, log_cols), out_shape...]
where the time goes in v6:
time: 102 us
  blocking collectives  88.4 us (87%)
  Pallas kernels  11.9 us (12%)
  between operations  1.32 us (1%)
    all_to_all x5, blocking collectives, exchange(): lax.all_to_all(x.reshape(parts, width), axis, 0, 0, axis_index_groups=gro...  88.4 us
    pallas_call x1, Pallas kernels, body(): pl.pallas_call(functools.partial(bary_kernel, n_row, log_cols), out_shape...  6.71 us
    pallas_call x1, Pallas kernels, body(): pl.pallas_call(functools.partial(src_kernel, other), out_shape=(rows_of(o...  2.34 us

profile of v6, /device:TPU:8, one launch (start us, length us, event | category | flops | bytes accessed | tf_op | source)
XLA Modules:
  0.0 101.6 jit_solution(1798826182085547791)
XLA Ops:
  1.3 2.3 %src_pass.1 = (f32[256,128]{1,0:T(8,128)S(1)}, bf16[8,96,512]{2,1,0:T(8,128)(2,1)S(1)}) custom-call(s32[1,1]{1,0:T(1,128)S(6)} %copy.13.count, s32[2,8]{1,0:T(2,128)} %bitcast.30, bf16[32,4096]{1,0:T(8,128)(2,1)} %x_ref.1, bf16[32,2048]{1,0:T(8,128)(2,1)} %y_ref.3, f32[1,2048]{1,0:T(1,128)} %bitcast.33), custom_call_target="tpu_custom_call" | custom-call | tf_op jit(solution)/shard_map/src_pass/pallas_call | solution.py:373
  3.6 20.2 %all_to_all.45 = f32[8,1,4096]{2,1,0:T(1,128)S(1)} all-to-all(f32[8,1,4096]{2,1,0:T(1,128)S(1)} %bitcast.27), channel_id=1, replica_groups={{0,8,16,24,32,40,48,56},{1,9,17,25,33,41,49,57},{2,10,18,26,34,42,50,58..., dimensions={0} | all-to-all | bytes 262144 | tf_op jit(solution)/shard_map/all_to_all | solution.py:365
  23.8 0.0 copy-start.1
  23.8 0.0 copy-start
  23.8 15.1 %all_to_all.46 = f32[8,1,4096]{2,1,0:T(1,128)S(1)} all-to-all(f32[8,1,4096]{2,1,0:T(1,128)S(1)} %bitcast.24), channel_id=1, replica_groups={{0,1,2,3,4,5,6,7},{8,9,10,11,12,13,14,15},{16,17,18,19,20,21,22,23},{24..., dimensions={0} | all-to-all | bytes 262144 | tf_op jit(solution)/shard_map/all_to_all | solution.py:365
  38.9 0.0 copy-done.1
  38.9 0.0 copy-done
  38.9 1.7 %tgt_pass.1 = (f32[32,128]{1,0:T(8,128)}, f32[128,128]{1,0:T(8,128)S(1)}) custom-call(s32[1,1]{1,0:T(1,128)S(6)} %copy.13.count, s32[2,8]{1,0:T(2,128)} %bitcast.31, f32[256,128]{1,0:T(8,128)S(1)} %bitcast.25, bf16[8,96,512]{2,1,0:T(8,128)(2,1)S(1)} %get-tuple-element.10.xs_ref, bf16[32,4096]{1,0:T(8,128)(2,1)S(1)} %copy-done.1, bf16[32,2048]{1,0:T(8,128)(2,1)S(1)} %copy-done), custom_call_target="tpu_custom_call" | custom-call | tf_op jit(solution)/shard_map/tgt_pass/pallas_call | solution.py:404
  40.7 9.7 %all_to_all.47 = f32[8,1,2048]{2,1,0:T(1,128)S(1)} all-to-all(f32[8,1,2048]{2,1,0:T(1,128)S(1)} %bitcast.28), channel_id=1, replica_groups=mesh['row'=8,'col'=64] {'row'}, dimensions={0} | all-to-all | bytes 131072 | tf_op jit(solution)/shard_map/all_to_all | solution.py:365
  50.4 6.7 %bary_pass.1 = (f32[16,128]{1,0:T(8,128)}, f32[1088,128]{1,0:T(8,128)S(1)}) custom-call(s32[1,1]{1,0:T(1,128)S(6)} %copy.13.count, s32[2,8]{1,0:T(2,128)} %bitcast.32, f32[128,128]{1,0:T(8,128)S(1)} %bitcast.26, bf16[8,96,512]{2,1,0:T(8,128)(2,1)S(1)} %get-tuple-element.10.xs_ref, bf16[32,2048]{1,0:T(8,128)(2,1)S(1)} %copy-done), custom_call_target="tpu_custom_call" | custom-call | tf_op jit(solution)/shard_map/bary_pass/pallas_call | solution.py:414
  57.2 23.1 %all_to_all.48 = f32[64,1,2176]{2,1,0:T(1,128)S(1)} all-to-all(f32[64,1,2176]{2,1,0:T(1,128)S(1)} %bitcast.22), channel_id=1, replica_groups=mesh['row'=8,'col'=64] {'col'}, dimensions={0} | all-to-all | bytes 1114112 | tf_op jit(solution)/shard_map/all_to_all | solution.py:365
  80.2 0.2 bary_merge.1
  80.4 20.3 %all_to_all.49 = f32[64,1,2048]{2,1,0:T(1,128)S(1)} all-to-all(f32[64,1,2048]{2,1,0:T(1,128)S(1)} %bitcast.20), channel_id=1, replica_groups=mesh['row'=8,'col'=64] {'col'}, dimensions={0} | all-to-all | bytes 1048576 | tf_op jit(solution)/shard_map/all_to_all | solution.py:365
  100.7 0.8 bary_place.1
  (1 shorter events, 0.0 us)
Async XLA Ops:
  23.8 15.2 %copy-start.1 = (bf16[32,4096]{1,0:T(8,128)(2,1)S(1)}, bf16[32,4096]{1,0:T(8,128)(2,1)}, u32[]{:S(2)}) copy-start(bf16[32,4096]{1,0:T(8,128)(2,1)} %x_ref.1) | copy-start | bytes 786436
  23.8 15.1 %copy-start = (bf16[32,2048]{1,0:T(8,128)(2,1)S(1)}, bf16[32,2048]{1,0:T(8,128)(2,1)}, u32[]{:S(2)}) copy-start(bf16[32,2048]{1,0:T(8,128)(2,1)} %y_ref.3) | copy-start | bytes 393220

commit v7 on v6

--- a/solution.py
+++ b/solution.py
@@ -251,7 +251,7 @@
     total_row = jnp.where(first_row, 1.0, 0.0).astype(BF16)
 
     def step(q, carry):
-        tiles = []
+        work = []
         for u in range(BARY_UNROLL):
             p = q * BARY_UNROLL + u
             live = p < count[0, 0]
@@ -259,15 +259,18 @@
             s, t = slots[0, p], slots[1, p]
             scores = tile_scores(tgt_operand(y_ref, t, bias_ref[t]), src_operand(xs_ref, s, ones))
             values = jnp.concatenate([tgt_block(y_ref, t), total_row], axis=0)
-            top = part = None
+            work.append([scores, values, None, None, jnp.where(live, s, spare)])
+        for item in work:
             for c in range(0, BLOCK, CHUNK):
+                scores, values, top, part, at = item
                 score = scores[c : c + CHUNK, :]
                 most = jnp.max(score, axis=0, keepdims=True)
                 old, top = top, most if c == 0 else jnp.maximum(top, most)
                 weight = jnp.exp2(score - top).astype(BF16)
                 more = jnp.dot(values[:, c : c + CHUNK], weight, preferred_element_type=F32)
                 part = more if c == 0 else part * jnp.exp2(old - top) + more
-            tiles.append((top, part, jnp.where(live, s, spare)))
+                item[2:4] = top, part
+        tiles = [item[2:] for item in work]
         for top, part, at in tiles:
             old = top_ref[at]
             most = jnp.maximum(old, top)

time: 102 us -> 101 us (level)
  blocking collectives: 88.4 us -> 84.1 us
  Pallas kernels: 11.9 us -> 15.7 us
    all_to_all x5, blocking collectives: 88.4 us -> 84.1 us  [exchange(): lax.all_to_all(x.reshape(parts, width), axis, 0, 0, axis_index_groups=gro...]
    pallas_call x1, Pallas kernels: 6.71 us -> 8.61 us  [body(): pl.pallas_call(functools.partial(bary_kernel, n_row, log_cols), out_shape...]
where the time goes in v7:
time: 101 us
  blocking collectives  84.1 us (83%)
  Pallas kernels  15.7 us (16%)
  between operations  1.32 us (1%)
    all_to_all x5, blocking collectives, exchange(): lax.all_to_all(x.reshape(parts, width), axis, 0, 0, axis_index_groups=gro...  84.1 us
    pallas_call x1, Pallas kernels, body(): pl.pallas_call(functools.partial(bary_kernel, n_row, log_cols), out_shape...  8.61 us
    pallas_call x1, Pallas kernels, body(): pl.pallas_call(functools.partial(src_kernel, other), out_shape=(rows_of(o...  3.3 us
    pallas_call x1, Pallas kernels, body(): pl.pallas_call(functools.partial(tgt_kernel, side, n_row, log_rows), out_...  2.7 us

profile of v7, /device:TPU:8, one launch (start us, length us, event | category | flops | bytes accessed | tf_op | source)
XLA Modules:
  0.0 101.1 jit_solution(16998041969116913487)
XLA Ops:
  1.3 3.3 %src_pass.1 = (f32[256,128]{1,0:T(8,128)S(1)}, bf16[8,96,512]{2,1,0:T(8,128)(2,1)S(1)}) custom-call(s32[1,1]{1,0:T(1,128)S(6)} %copy.13.count, s32[2,8]{1,0:T(2,128)} %bitcast.30, bf16[32,4096]{1,0:T(8,128)(2,1)} %x_ref.1, bf16[32,2048]{1,0:T(8,128)(2,1)} %y_ref.3, f32[1,2048]{1,0:T(1,128)} %bitcast.33), custom_call_target="tpu_custom_call" | custom-call | tf_op jit(solution)/shard_map/src_pass/pallas_call | solution.py:376
  4.6 19.2 %all_to_all.45 = f32[8,1,4096]{2,1,0:T(1,128)S(1)} all-to-all(f32[8,1,4096]{2,1,0:T(1,128)S(1)} %bitcast.27), channel_id=1, replica_groups={{0,8,16,24,32,40,48,56},{1,9,17,25,33,41,49,57},{2,10,18,26,34,42,50,58..., dimensions={0} | all-to-all | bytes 262144 | tf_op jit(solution)/shard_map/all_to_all | solution.py:368
  23.8 0.0 copy-start.1
  23.8 0.0 copy-start
  23.9 14.1 %all_to_all.46 = f32[8,1,4096]{2,1,0:T(1,128)S(1)} all-to-all(f32[8,1,4096]{2,1,0:T(1,128)S(1)} %bitcast.24), channel_id=1, replica_groups={{0,1,2,3,4,5,6,7},{8,9,10,11,12,13,14,15},{16,17,18,19,20,21,22,23},{24..., dimensions={0} | all-to-all | bytes 262144 | tf_op jit(solution)/shard_map/all_to_all | solution.py:368
  38.0 0.0 copy-done.1
  38.0 0.0 copy-done
  38.0 2.7 %tgt_pass.1 = (f32[32,128]{1,0:T(8,128)}, f32[128,128]{1,0:T(8,128)S(1)}) custom-call(s32[1,1]{1,0:T(1,128)S(6)} %copy.13.count, s32[2,8]{1,0:T(2,128)} %bitcast.31, f32[256,128]{1,0:T(8,128)S(1)} %bitcast.25, bf16[8,96,512]{2,1,0:T(8,128)(2,1)S(1)} %get-tuple-element.10.xs_ref, bf16[32,4096]{1,0:T(8,128)(2,1)S(1)} %copy-done.1, bf16[32,2048]{1,0:T(8,128)(2,1)S(1)} %copy-done), custom_call_target="tpu_custom_call" | custom-call | tf_op jit(solution)/shard_map/tgt_pass/pallas_call | solution.py:407
  40.7 9.7 %all_to_all.47 = f32[8,1,2048]{2,1,0:T(1,128)S(1)} all-to-all(f32[8,1,2048]{2,1,0:T(1,128)S(1)} %bitcast.28), channel_id=1, replica_groups=mesh['row'=8,'col'=64] {'row'}, dimensions={0} | all-to-all | bytes 131072 | tf_op jit(solution)/shard_map/all_to_all | solution.py:368
  50.4 8.6 %bary_pass.1 = (f32[16,128]{1,0:T(8,128)}, f32[1088,128]{1,0:T(8,128)S(1)}) custom-call(s32[1,1]{1,0:T(1,128)S(6)} %copy.13.count, s32[2,8]{1,0:T(2,128)} %bitcast.32, f32[128,128]{1,0:T(8,128)S(1)} %bitcast.26, bf16[8,96,512]{2,1,0:T(8,128)(2,1)S(1)} %get-tuple-element.10.xs_ref, bf16[32,2048]{1,0:T(8,128)(2,1)S(1)} %copy-done), custom_call_target="tpu_custom_call" | custom-call | tf_op jit(solution)/shard_map/bary_pass/pallas_call | solution.py:417
  59.0 20.3 %all_to_all.48 = f32[64,1,2176]{2,1,0:T(1,128)S(1)} all-to-all(f32[64,1,2176]{2,1,0:T(1,128)S(1)} %bitcast.22), channel_id=1, replica_groups=mesh['row'=8,'col'=64] {'col'}, dimensions={0} | all-to-all | bytes 1114112 | tf_op jit(solution)/shard_map/all_to_all | solution.py:368
  79.3 0.2 bary_merge.1
  79.5 20.8 %all_to_all.49 = f32[64,1,2048]{2,1,0:T(1,128)S(1)} all-to-all(f32[64,1,2048]{2,1,0:T(1,128)S(1)} %bitcast.20), channel_id=1, replica_groups=mesh['row'=8,'col'=64] {'col'}, dimensions={0} | all-to-all | bytes 1048576 | tf_op jit(solution)/shard_map/all_to_all | solution.py:368
  100.3 0.8 bary_place.1
  (1 shorter events, 0.0 us)
Async XLA Ops:
  23.8 14.2 %copy-start.1 = (bf16[32,4096]{1,0:T(8,128)(2,1)S(1)}, bf16[32,4096]{1,0:T(8,128)(2,1)}, u32[]{:S(2)}) copy-start(bf16[32,4096]{1,0:T(8,128)(2,1)} %x_ref.1) | copy-start | bytes 786436
  23.8 14.2 %copy-start = (bf16[32,2048]{1,0:T(8,128)(2,1)S(1)}, bf16[32,2048]{1,0:T(8,128)(2,1)}, u32[]{:S(2)}) copy-start(bf16[32,2048]{1,0:T(8,128)(2,1)} %y_ref.3) | copy-start | bytes 393220

commit v8 on v7

--- a/solution.py
+++ b/solution.py
@@ -159,14 +159,15 @@
         (x_in, y_in, g_in, slots_in), (x_ref, y_ref, g_ref, slots), sems
     )
     clear(top_ref, total_ref)
-    for copy in copies:
+    for copy in copies[1:]:
         copy.wait()
-    fill_src(x_ref, xs_ref)
     for b in range(bias_ref.shape[0]):
         ys = y_ref[:, b * BLOCK : (b + 1) * BLOCK].astype(F32)
         square = jnp.sum(ys * ys, axis=0, keepdims=True)
         start = g_ref[:, b * BLOCK : (b + 1) * BLOCK]
         bias_ref[b] = bias_rows(start / unit - square * square_scale)
+    copies[0].wait()
+    fill_src(x_ref, xs_ref)
     ones = one_rows(BLOCK)
     blocks = xs_ref.shape[0]
     lse_tiles(
@@ -267,7 +268,7 @@
                 most = jnp.max(score, axis=0, keepdims=True)
                 old, top = top, most if c == 0 else jnp.maximum(top, most)
                 weight = jnp.exp2(score - top).astype(BF16)
-                more = jnp.dot(values[:, c : c + CHUNK], weight, preferred_element_type=F32)
+                more = jnp.dot(values[:, c : c + CHUNK], weight, preferred_element_type=F32)[0:40, :]
                 part = more if c == 0 else part * jnp.exp2(old - top) + more
                 item[2:4] = top, part
         tiles = [item[2:] for item in work]
@@ -423,7 +424,7 @@
             *side_refs(t_rows),
             tails(t_blocks),
             line(s_blocks + 1, 1),
-            pltpu.VMEM((s_blocks + 1, 48, BLOCK), F32),
+            pltpu.VMEM((s_blocks + 1, 40, BLOCK), F32),
         ],
         compiler_params=pltpu.CompilerParams(vmem_limit_bytes=VMEM_LIMIT),
         name="bary_pass",

time: 101 us -> 101 us (level)
  blocking collectives: 84.1 us -> 87.5 us
  Pallas kernels: 15.7 us -> 12.3 us
    all_to_all x5, blocking collectives: 84.1 us -> 87.5 us  [exchange(): lax.all_to_all(x.reshape(parts, width), axis, 0, 0, axis_index_groups=gro...]
    pallas_call x1, Pallas kernels: 8.61 us -> 7.19 us  [body(): pl.pallas_call(functools.partial(bary_kernel, n_row, log_cols), out_shape...]
where the time goes in v8:
time: 101 us
  blocking collectives  87.5 us (87%)
  Pallas kernels  12.3 us (12%)
  between operations  1.32 us (1%)
    all_to_all x5, blocking collectives, exchange(): lax.all_to_all(x.reshape(parts, width), axis, 0, 0, axis_index_groups=gro...  87.5 us
    pallas_call x1, Pallas kernels, body(): pl.pallas_call(functools.partial(bary_kernel, n_row, log_cols), out_shape...  7.19 us
    pallas_call x1, Pallas kernels, body(): pl.pallas_call(functools.partial(src_kernel, other), out_shape=(rows_of(o...  2.34 us

profile of v8, /device:TPU:8, one launch (start us, length us, event | category | flops | bytes accessed | tf_op | source)
XLA Modules:
  0.0 101.2 jit_solution(4731334693978945891)
XLA Ops:
  1.3 2.3 %src_pass.1 = (f32[256,128]{1,0:T(8,128)S(1)}, bf16[8,96,512]{2,1,0:T(8,128)(2,1)S(1)}) custom-call(s32[1,1]{1,0:T(1,128)S(6)} %copy.13.count, s32[2,8]{1,0:T(2,128)} %bitcast.30, bf16[32,4096]{1,0:T(8,128)(2,1)} %x_ref.1, bf16[32,2048]{1,0:T(8,128)(2,1)} %y_ref.3, f32[1,2048]{1,0:T(1,128)} %bitcast.33), custom_call_target="tpu_custom_call" | custom-call | tf_op jit(solution)/shard_map/src_pass/pallas_call | solution.py:377
  3.6 20.2 %all_to_all.45 = f32[8,1,4096]{2,1,0:T(1,128)S(1)} all-to-all(f32[8,1,4096]{2,1,0:T(1,128)S(1)} %bitcast.27), channel_id=1, replica_groups={{0,8,16,24,32,40,48,56},{1,9,17,25,33,41,49,57},{2,10,18,26,34,42,50,58..., dimensions={0} | all-to-all | bytes 262144 | tf_op jit(solution)/shard_map/all_to_all | solution.py:369
  23.8 0.0 copy-start.1
  23.8 0.0 copy-start
  23.8 14.3 %all_to_all.46 = f32[8,1,4096]{2,1,0:T(1,128)S(1)} all-to-all(f32[8,1,4096]{2,1,0:T(1,128)S(1)} %bitcast.24), channel_id=1, replica_groups={{0,1,2,3,4,5,6,7},{8,9,10,11,12,13,14,15},{16,17,18,19,20,21,22,23},{24..., dimensions={0} | all-to-all | bytes 262144 | tf_op jit(solution)/shard_map/all_to_all | solution.py:369
  38.1 0.0 copy-done.1
  38.1 0.0 copy-done
  38.2 1.7 %tgt_pass.1 = (f32[32,128]{1,0:T(8,128)}, f32[128,128]{1,0:T(8,128)S(1)}) custom-call(s32[1,1]{1,0:T(1,128)S(6)} %copy.13.count, s32[2,8]{1,0:T(2,128)} %bitcast.31, f32[256,128]{1,0:T(8,128)S(1)} %bitcast.25, bf16[8,96,512]{2,1,0:T(8,128)(2,1)S(1)} %get-tuple-element.10.xs_ref, bf16[32,4096]{1,0:T(8,128)(2,1)S(1)} %copy-done.1, bf16[32,2048]{1,0:T(8,128)(2,1)S(1)} %copy-done), custom_call_target="tpu_custom_call" | custom-call | tf_op jit(solution)/shard_map/tgt_pass/pallas_call | solution.py:408
  39.9 11.5 %all_to_all.47 = f32[8,1,2048]{2,1,0:T(1,128)S(1)} all-to-all(f32[8,1,2048]{2,1,0:T(1,128)S(1)} %bitcast.28), channel_id=1, replica_groups=mesh['row'=8,'col'=64] {'row'}, dimensions={0} | all-to-all | bytes 131072 | tf_op jit(solution)/shard_map/all_to_all | solution.py:369
  51.4 7.2 %bary_pass.1 = (f32[16,128]{1,0:T(8,128)}, f32[1088,128]{1,0:T(8,128)S(1)}) custom-call(s32[1,1]{1,0:T(1,128)S(6)} %copy.13.count, s32[2,8]{1,0:T(2,128)} %bitcast.32, f32[128,128]{1,0:T(8,128)S(1)} %bitcast.26, bf16[8,96,512]{2,1,0:T(8,128)(2,1)S(1)} %get-tuple-element.10.xs_ref, bf16[32,2048]{1,0:T(8,128)(2,1)S(1)} %copy-done), custom_call_target="tpu_custom_call" | custom-call | tf_op jit(solution)/shard_map/bary_pass/pallas_call | solution.py:418
  58.6 20.9 %all_to_all.48 = f32[64,1,2176]{2,1,0:T(1,128)S(1)} all-to-all(f32[64,1,2176]{2,1,0:T(1,128)S(1)} %bitcast.22), channel_id=1, replica_groups=mesh['row'=8,'col'=64] {'col'}, dimensions={0} | all-to-all | bytes 1114112 | tf_op jit(solution)/shard_map/all_to_all | solution.py:369
  79.5 0.2 bary_merge.1
  79.7 20.6 %all_to_all.49 = f32[64,1,2048]{2,1,0:T(1,128)S(1)} all-to-all(f32[64,1,2048]{2,1,0:T(1,128)S(1)} %bitcast.20), channel_id=1, replica_groups=mesh['row'=8,'col'=64] {'col'}, dimensions={0} | all-to-all | bytes 1048576 | tf_op jit(solution)/shard_map/all_to_all | solution.py:369
  100.3 0.8 bary_place.1
  (1 shorter events, 0.0 us)
Async XLA Ops:
  23.8 14.4 %copy-start.1 = (bf16[32,4096]{1,0:T(8,128)(2,1)S(1)}, bf16[32,4096]{1,0:T(8,128)(2,1)}, u32[]{:S(2)}) copy-start(bf16[32,4096]{1,0:T(8,128)(2,1)} %x_ref.1) | copy-start | bytes 786436
  23.8 14.3 %copy-start = (bf16[32,2048]{1,0:T(8,128)(2,1)S(1)}, bf16[32,2048]{1,0:T(8,128)(2,1)}, u32[]{:S(2)}) copy-start(bf16[32,2048]{1,0:T(8,128)(2,1)} %y_ref.3) | copy-start | bytes 393220
